TPU v7x, 256 devices: a whole 4x4x8 slice. The times are simulated.
256 devices in a mesh: dom: 128 (over x, y, z), feat: 2 (over core).
Axes of the slice: x: 4, y: 4, z: 8, core: 2. Of those that a mesh axis runs over, the one named last changes fastest.
Arguments:
- history: bfloat16 [131072, 256], P('dom', 'feat'), may hold values from -6 to 6
- pull_list: int32 [128, 128, 2], P('dom'), may hold values from -1 to 7, as said below
- remote_tiles: bfloat16 [128, 128, 2, 128, 128], P('dom'), may hold values from -0.1875 to 0.1875
- remote_dst: int32 [128, 128, 2], P('dom'), may hold values from 0 to 15
- local_tiles: bfloat16 [8192, 128, 128], P('dom'), may hold values from -0.1875 to 0.1875
- local_src: int32 [128, 64], P('dom'), may hold values from 0 to 7
- local_dst: int32 [128, 64], P('dom'), may hold values from 0 to 15
- weight: bfloat16 [256, 256], P(None, 'feat'), may hold values from -0.375 to 0.375
- bias: float32 [256], P('feat'), may hold values from -3 to 3
- cotangent: bfloat16 [131072, 256], P('dom', 'feat'), may hold values from -0.015625 to 0.015625
Outputs:
- new_rows: bfloat16 [131072, 256], P('dom', 'feat')
- grad_weight: float32 [256, 256], P(None, 'feat')
- grad_bias: float32 [256], P('feat')
Inputs may be any that keep to these rules, and one draw needn't show every extreme that they name: pull_list[r, o, c] is -1 or a block index local to owner o; in each (r, o) the used entries come first and are distinct; pull_list[r, r] is all -1; every other (r, o) asks 2 or 1 blocks; every partition asks 2 blocks of the next partition, and some owner is asked for 2 blocks by every other partition.
All inputs are finite; a program needn't handle non-finite values.
Results may differ from a plain program's by a relative error of at most 0.0065.
Values may be sent and summed in bfloat16 or wider, within the bound.
A program may use at most 128 MiB of HBM per device.

v0:
```python
import jax
import jax.numpy as jnp
from jax import lax
from jax.sharding import PartitionSpec as P


def passed_along(block, axis, distance):
    devices = range(lax.axis_size(axis))
    route = [((i - distance) % len(devices), i) for i in devices]
    return lax.ppermute(block, axis, route)


def activate(value):
    return jax.nn.gelu(value, approximate=True)


def select_rows(targets, row_count, values):
    one_hot = (
        targets.reshape(-1)[None, :] == jnp.arange(row_count, dtype=jnp.int32)[:, None]
    ).astype(jnp.float32)
    return jnp.dot(one_hot, values, precision=lax.Precision.HIGHEST)


def per_device(
    history,
    pull_list,
    remote_tiles,
    remote_dst,
    local_tiles,
    local_src,
    local_dst,
    weight,
    bias,
    cotangent,
):
    half_width = history.shape[1]
    block_size = local_tiles.shape[1]
    own_blocks = history.shape[0] // block_size
    row_count = 2 * own_blocks
    blocks = history.reshape(own_blocks, block_size, half_width)
    requested = pull_list[0]
    asked = lax.all_to_all(requested, "dom", split_axis=0, concat_axis=0, tiled=True)
    clamped = jnp.clip(asked, 0, own_blocks - 1)
    picked = blocks[clamped]
    pulled = lax.all_to_all(
        jnp.where((asked >= 0)[:, :, None, None], picked, jnp.zeros((), history.dtype)),
        "dom",
        split_axis=0,
        concat_axis=0,
        tiled=True,
    )
    sources = blocks[local_src[0]]
    local_prod = jnp.einsum(
        "kij,kjf->kif", local_tiles, sources, preferred_element_type=jnp.float32
    )
    partial_value = select_rows(
        local_dst[0], row_count, local_prod.reshape(-1, block_size * half_width)
    )
    products = jnp.einsum(
        "ockj,ocjf->ockf", remote_tiles[0], pulled, preferred_element_type=jnp.float32
    )
    partial_value = partial_value + select_rows(
        remote_dst[0], row_count, products.reshape(-1, block_size * half_width)
    )
    incoming = passed_along(partial_value[own_blocks:], "dom", 1)
    aggregate = (
        (partial_value[:own_blocks] + incoming)
        .reshape(own_blocks * block_size, half_width)
        .astype(jnp.bfloat16)
    )
    aggregate_full = lax.all_gather(aggregate, "feat", axis=1, tiled=True)
    preact = jnp.dot(aggregate_full, weight, preferred_element_type=jnp.float32) + bias
    new_rows, backward_fn = jax.vjp(activate, preact)
    grad_pre = backward_fn(cotangent.astype(jnp.float32))[0].astype(jnp.bfloat16)
    weight_term = lax.dot_general(
        aggregate_full, grad_pre, (((0,), (0,)), ((), ())), preferred_element_type=jnp.float32
    )
    bias_term = jnp.sum(grad_pre.astype(jnp.float32), axis=0)
    grad_weight, grad_bias = lax.psum((weight_term, bias_term), "dom")
    return (new_rows.astype(jnp.bfloat16), grad_weight, grad_bias)


def solution(mesh):
    placed = (
        P("dom", "feat"),
        P("dom", None, None),
        P("dom", None, None, None, None),
        P("dom", None, None),
        P("dom", None, None),
        P("dom", None),
        P("dom", None),
        P(None, "feat"),
        P("feat"),
        P("dom", "feat"),
    )
    return jax.shard_map(
        per_device,
        mesh=mesh,
        in_specs=placed,
        out_specs=(P("dom", "feat"), P(None, "feat"), P("feat")),
        check_vma=False,
    )
```

profile of v0, /device:TPU:32, one launch (start us, length us, event | category | flops | bytes accessed | tf_op | source)
XLA Modules:
  0.0 684.6 jit_solution(4032542416159251060)
XLA Ops:
  7.2 0.0 copy-start
  7.2 0.9 copy.30
  8.1 26.0 %all_to_all.14 = s32[128,1,2]{2,1,0:T(1,128)S(1)} all-to-all(s32[128,1,2]{2,1,0:T(1,128)S(1)} %bitcast.40), channel_id=1, replica_groups=mesh['dom'=128,'feat'=2] {'dom'}, dimensions={0} | all-to-all | bytes 2048 | tf_op jit(solution)/shard_map/all_to_all | solution.py:42
  34.1 0.1 broadcast_clamp_fusion
  34.2 0.1 reshape.92
  34.3 9.5 %gather_fusion.1 = bf16[256,128,128]{2,1,0:T(8,128)(2,1)} fusion(bf16[8,128,128]{2,1,0:T(8,128)(2,1)} %bitcast.35, s32[1024]{0:T(1024)S(1)} %pad_clamp_fusion), kind=kCustom, calls=%fused_computation.1 | custom fusion | bytes 16778240 | tf_op jit(solution)/shard_map/gather | solution.py:44
  43.9 11.9 %copy.33 = bf16[256,128,128]{1,2,0:T(8,128)(2,1)} copy(bf16[256,128,128]{2,1,0:T(8,128)(2,1)} %gather_fusion.1) | data formatting | bytes 16777216 | tf_op jit(solution)/shard_map/gather | solution.py:44
  55.8 0.1 broadcast_compare_fusion
  55.9 0.1 copy.31
  56.0 0.1 copy.32
  56.1 7.3 %broadcast_select_fusion = bf16[128,2,128,128]{2,3,1,0:T(8,128)(2,1)} fusion(bf16[128,2,128,128]{2,3,1,0:T(8,128)(2,1)} %bitcast.38, pred[128,2]{1,0:T(8,128)(4,1)S(1)} %copy.32), kind=kLoop, calls=%fused_computation.7 | loop fusion | flops 4194304 | bytes 16777472 | tf_op jit(solution)/shard_map/jit(_where)/select_n | solution.py:46
  63.4 0.0 copy-start.7
  63.4 0.0 copy-start.2
  63.4 8.0 %all-to-all-start.1 = ((bf16[128,2,128,128]{2,3,1,0:T(8,128)(2,1)}), bf16[128,2,128,128]{2,3,1,0:T(8,128)(2,1)}, u32[]{:S(2)}, u32[]{:S(2)}) async-start(bf16[128,2,128,128]{2,3,1,0:T(8,128)(2,1)} %broadcast_select_fusion), calls=%async_computation.1 | async-start | bytes 16777216 | tf_op jit(solution)/shard_map/all_to_all | solution.py:45
  71.4 0.2 all-reduce.2.cloned.1.call-start
  71.7 0.0 copy-done.7
  71.7 0.0 copy-done.2
  71.7 2.1 gather_fusion
  73.8 0.0 copy-done
  73.8 0.0 copy-start.3
  73.8 0.0 copy-start.4
  73.9 5.2 convolution_bitcast_fusion.1
  79.0 5.6 copy.28
  84.7 0.0 copy-done.3
  84.7 0.1 copy.29
  84.8 0.1 eq.34
  84.9 0.0 copy-done.4
  84.9 5.8 fusion.3
  90.7 168.0 %all-to-all-done.1 = bf16[128,2,128,128]{2,3,1,0:T(8,128)(2,1)} async-done(((bf16[128,2,128,128]{2,3,1,0:T(8,128)(2,1)}), bf16[128,2,128,128]{2,3,1,0:T(8,128)(2,1)}, u32[]{:S(2)}, u32[]{:S(2)}) %all-to-all-start.1) | async-done | bytes 8388640 | tf_op jit(solution)/shard_map/all_to_all | solution.py:45
  258.7 17.4 %convolution_bitcast_fusion = f32[128,2,128,128]{2,3,1,0:T(8,128)} fusion(bf16[128,2,128,128]{2,3,1,0:T(8,128)(2,1)} %all-to-all-done.1, bf16[1,128,2,128,128]{4,3,2,1,0:T(8,128)(2,1)} %param.12), kind=kOutput, calls=%fused_computation.5 | convolution fusion | flops 1073741824 | bytes 33554432 | tf_op jit(solution)/shard_map/ockj,ocjf->ockf/dot_general | solution.py:59
  276.1 17.4 %copy.34 = f32[128,2,128,128]{3,2,1,0:T(8,128)} copy(f32[128,2,128,128]{2,3,1,0:T(8,128)} %convolution_bitcast_fusion) | data formatting | bytes 33554432 | tf_op jit(solution)/shard_map/ockj,ocjf->ockf/dot_general | solution.py:59
  293.5 0.0 copy-start.5
  293.5 0.0 copy-start.6
  293.6 0.0 copy-start.1
  293.6 20.4 %convolution_add_fusion = f32[16,16384]{1,0:T(8,128)S(1)} fusion(f32[16,16384]{1,0:T(8,128)S(1)} %fusion.3, f32[32,8,128,128]{3,2,1,0:T(8,128)} %bitcast.37, s32[256]{0:T(256)S(1)} %eq.34), kind=kOutput, calls=%fused_computation.2 | convolution fusion | flops 805572608 | bytes 18875392 | tf_op jit(solution)/shard_map/dot_general | solution.py:21
  314.0 0.1 collective-permute-start
  314.1 11.8 %collective-permute-done = f32[8,16384]{1,0:T(8,128)S(1)} collective-permute-done((f32[8,16384]{1,0:T(8,128)S(1)}, f32[8,16384]{1,0:T(8,128)S(1)}, u32[]{:S(2)}, u32[]{:S(2)}) %collective-permute-start) | collective-permute-done | bytes 524320 | tf_op jit(solution)/shard_map/ppermute | solution.py:10
  325.9 0.1 convert_element_type.21
  326.0 2.2 all_gather.3
  328.3 0.0 copy-done.5
  328.3 0.0 copy-done.6
  328.3 0.0 copy-done.8
  328.3 1.3 convert_reduce_fusion
  329.6 1.0 fusion.21
  330.6 0.0 all-reduce.2.cloned.1.call-update
  330.6 345.6 %psum.15 = f32[128]{0:T(128)} all-reduce(f32[128]{0:T(128)S(1)} %get-tuple-element.3), channel_id=1, replica_groups=mesh['dom'=128,'feat'=2] {'dom'}, use_global_device_ids=true, to_apply=%region_2.3 | all-reduce | flops 128 | bytes 1024 | tf_op jit(solution)/shard_map/psum | solution.py:79
  676.2 1.6 copy.47
  677.8 0.0 copy-done.1
  (8 shorter events, 0.1 us)
Async XLA Ops:
  7.2 66.7 %copy-start = (bf16[64,128,128]{2,1,0:T(8,128)(2,1)S(1)}, bf16[64,128,128]{2,1,0:T(8,128)(2,1)}, u32[]{:S(2)}) copy-start(bf16[64,128,128]{2,1,0:T(8,128)(2,1)} %param.14) | copy-start | bytes 6291460
  63.4 8.3 %copy-start.7 = (s32[1,64]{1,0:T(1,128)S(1)}, s32[1,64]{1,0:T(1,128)}, u32[]{:S(2)}) copy-start(s32[1,64]{1,0:T(1,128)} %param.15) | copy-start | bytes 772
  63.4 8.3 %copy-start.2 = (bf16[1024,128]{1,0:T(8,128)(2,1)S(1)}, bf16[1024,128]{1,0:T(8,128)(2,1)}, u32[]{:S(2)}) copy-start(bf16[1024,128]{1,0:T(8,128)(2,1)} %param.10) | copy-start | bytes 786436
  63.4 195.3 %all-to-all-start.1 = ((bf16[128,2,128,128]{2,3,1,0:T(8,128)(2,1)}), bf16[128,2,128,128]{2,3,1,0:T(8,128)(2,1)}, u32[]{:S(2)}, u32[]{:S(2)}) async-start(bf16[128,2,128,128]{2,3,1,0:T(8,128)(2,1)} %broadcast_select_fusion), calls=%async_computation.1 | async-start | bytes 16777216 | tf_op jit(solution)/shard_map/all_to_all | solution.py:45
  71.4 604.8 %all-reduce.2.cloned.1.call-start = ((), (), s32[]{:S(2)}) async-start(), calls=%async_computation.2 | async-start | bytes 262144 | tf_op jit(solution)/shard_map/psum | solution.py:79
  73.8 10.8 %copy-start.3 = (s32[1,128,2]{1,2,0:T(2,128)S(1)}, s32[1,128,2]{1,2,0:T(2,128)}, u32[]{:S(2)}) copy-start(s32[1,128,2]{1,2,0:T(2,128)} %param.13) | copy-start | bytes 3076
  73.8 11.1 %copy-start.4 = (s32[1,64]{1,0:T(1,128)S(1)}, s32[1,64]{1,0:T(1,128)}, u32[]{:S(2)}) copy-start(s32[1,64]{1,0:T(1,128)} %param.16) | copy-start | bytes 772
  293.5 34.7 %copy-start.5 = (bf16[1024,128]{1,0:T(8,128)(2,1)S(1)}, bf16[1024,128]{1,0:T(8,128)(2,1)}, u32[]{:S(2)}) copy-start(bf16[1024,128]{1,0:T(8,128)(2,1)} %param.19) | copy-start | bytes 786436
  293.5 34.7 %copy-start.6 = (bf16[256,128]{1,0:T(8,128)(2,1)S(1)}, bf16[256,128]{1,0:T(8,128)(2,1)}, u32[]{:S(2)}) copy-start(bf16[256,128]{1,0:T(8,128)(2,1)} %param.17) | copy-start | bytes 196612
  293.6 34.7 %copy-start.8 = (f32[128]{0:T(128)S(1)}, f32[128]{0:T(128)}, u32[]{:S(2)}) copy-start(f32[128]{0:T(128)} %param.18) | copy-start | bytes 1540
  293.6 384.2 %copy-start.1 = (bf16[64,128,128]{2,1,0:T(8,128)(2,1)S(1)}, bf16[64,128,128]{2,1,0:T(8,128)(2,1)}, u32[]{:S(2)}) copy-start(bf16[64,128,128]{2,1,0:T(8,128)(2,1)} %param.14) | copy-start | bytes 6291460
  314.0 11.9 %collective-permute-start = (f32[8,16384]{1,0:T(8,128)S(1)}, f32[8,16384]{1,0:T(8,128)S(1)}, u32[]{:S(2)}, u32[]{:S(2)}) collective-permute-start(f32[8,16384]{1,0:T(8,128)S(1)} %slice.13), channel_id=1, source_target_pairs={{254,0},{0,2},{2,4},{4,6},{6,8},{8,10},{10,12},{12,14},{14,16},{16... | collective-permute-start | bytes 1572872 | tf_op jit(solution)/shard_map/ppermute | solution.py:10
Sparse Core Ops, SparseCore 0:
  330.7 207.1 all-reduce.1
where the time goes:
time: 686 us; the launch traced here: 685 us
  blocking collectives  374 us (55%)
  waiting for transfers between devices  180 us (26%)
  matrix products  51.1 us (7%)
  local copies, waits for them, and re-layouts  50 us (7%)
  between operations  14.2 us (2%)
  starting transfers between devices  8.32 us (1%)
  other arithmetic  7.52 us (1%)
    psum x1, blocking collectives, per_device(): grad_weight, grad_bias = lax.psum((weight_term, bias_term), 'dom')  346 us
    all_to_all x1, waiting for transfers between devices, per_device(): lax.all_to_all(jnp.where((asked >= 0)[:, :, None, None], picked, jnp.zero...  168 us
    dot_general x2, matrix products, select_rows(): return jnp.dot(one_hot, values, precision=lax.Precision.HIGHEST)  26.2 us
    all_to_all x1, blocking collectives, per_device(): lax.all_to_all(requested, 'dom', split_axis=0, concat_axis=0, tiled=True)  26 us
    gather x2, local copies, waits for them, and re-layouts, per_device(): picked = blocks[clamped]  21.4 us
    dot_general x1, local copies, waits for them, and re-layouts, per_device(): jnp.einsum('ockj,ocjf->ockf', remote_tiles[0], pulled, preferred_element_...  17.4 us
    dot_general x1, matrix products, per_device(): jnp.einsum('ockj,ocjf->ockf', remote_tiles[0], pulled, preferred_element_...  17.4 us
  transfers between devices with their start and end apart: 3, of which 2 were waited for; matrix products, arithmetic and copies ran while one was open for 3% of the time, Pallas kernels for 0%

commit v1 on v0

v1 whole, which is shorter than its diff:
```python
import functools

import jax
import jax.numpy as jnp
from jax import lax
from jax.sharding import PartitionSpec as P
from jax.experimental import pallas as pl
from jax.experimental.pallas import tpu as pltpu

MESH = pl.DeviceIdType.MESH
X, Y, Z = 0, 1, 2
SIZES = (4, 4, 8)
STRIDES = (32, 8, 1)
NB = 8
BLK = 128
HALF = 128
SLICE = 32
KINDS = ((Z, Y, X), (Z, X, Y), (Y, Z, X), (X, Z, Y))


def coords():
    p = lax.axis_index("dom")
    return (p // 32, lax.rem(p // 8, 4), lax.rem(p, 8)), lax.axis_index("feat")


def moved(me, axis, offset):
    n = SIZES[axis]
    there = list(me)
    there[axis] = lax.rem(me[axis] + (offset % n), n)
    return there[0] * 32 + there[1] * 8 + there[2]


def pull_kernel(hist, plist, pulled, *scratch):
    sets = [scratch[0:4], scratch[4:8], scratch[8:16], scratch[16:24]]
    packs = scratch[24:28]
    lists_v, lists_s, send_sems, recv_sems, local_sems = scratch[28:33]
    me, f = coords()
    used = [0, 0]
    remote_copies = []
    local_copies = []

    def remote(src, dst, axis, offset):
        i = used[0]
        used[0] += 1
        copy = pltpu.make_async_remote_copy(
            src_ref=src,
            dst_ref=dst,
            send_sem=send_sems.at[i],
            recv_sem=recv_sems.at[i],
            device_id=(moved(me, axis, offset), f),
            device_id_type=MESH,
        )
        copy.start()
        remote_copies.append(copy)
        return copy

    def local(src, dst):
        i = used[1]
        used[1] += 1
        copy = pltpu.make_async_copy(src, dst, local_sems.at[i])
        copy.start()
        local_copies.append(copy)
        return copy

    def own(t):
        return hist.at[:, pl.ds(SLICE * t, SLICE), :]

    barrier = pltpu.get_barrier_semaphore()
    partners = [(X, 1), (X, 2), (X, 3), (Y, 1), (Y, 2), (Y, 3), (Z, 1), (Z, 7)]
    for axis, offset in partners:
        pl.semaphore_signal(
            barrier, inc=1, device_id=(moved(me, axis, offset), f), device_id_type=MESH
        )
    pl.semaphore_wait(barrier, len(partners))

    z_in = {}
    mid_in = {}
    for t in (0, 1):
        for d in (1, -1):
            z_in[t, d] = remote(own(t), sets[t][0].at[d % 8], Z, d)
    for t in (2, 3):
        a = KINDS[t][0]
        for d in (1, -1):
            mid_in[t, d] = remote(own(t), sets[t][0].at[d % 4], a, d)
    for t in (0, 1):
        b = KINDS[t][1]
        for d in (1, -1):
            mid_in[t, d, 0] = remote(own(t), sets[t][d % 4].at[0], b, d)
    list_in = []
    for i, axis in enumerate((X, Y)):
        for k in (1, 2, 3):
            list_in.append(remote(plist, lists_v.at[3 * i + k], axis, -k))
    for t in range(4):
        sets[t][0][0] = hist[:, SLICE * t : SLICE * (t + 1), :]
    lists_v[0] = plist[...]

    def half_forward_first(t):
        a = KINDS[t][0]
        ring = sets[t][0]
        mid_in[t, 1].wait_recv()
        p = remote(ring.at[1, pl.ds(0, 4)], ring.at[2, pl.ds(0, 4)], a, 1)
        mid_in[t, -1].wait_recv()
        q = remote(ring.at[3, pl.ds(4, 4)], ring.at[2, pl.ds(4, 4)], a, -1)
        mid_in[t, 2] = (p, q)

    reach = {0: (3, 4), 1: (4, 3), 2: (4, 3), 3: (3, 4)}

    def z_arrival(t, h):
        z_in[t, h].wait_recv()
        d = 1 if h > 0 else -1
        limit = reach[t][0] if h > 0 else reach[t][1]
        here = sets[t][0].at[h % 8]
        if abs(h) < limit:
            z_in[t, h + d] = remote(here, sets[t][0].at[(h + d) % 8], Z, d)
        for e in (1, -1):
            mid_in[t, e, h] = remote(here, sets[t][e % 4].at[h % 8], KINDS[t][1], e)

    def half_forward(t, h):
        b = KINDS[t][1]
        mid_in[t, 1, h].wait_recv()
        p = remote(
            sets[t][1].at[h % 8, pl.ds(0, 4)], sets[t][2].at[h % 8, pl.ds(0, 4)], b, 1
        )
        mid_in[t, -1, h].wait_recv()
        q = remote(
            sets[t][3].at[h % 8, pl.ds(4, 4)], sets[t][2].at[h % 8, pl.ds(4, 4)], b, -1
        )
        mid_in[t, 2, h] = (p, q)

    wide_in = {}

    def wide_start(t):
        for copy in mid_in[t, 2]:
            copy.wait_recv()
        for d in (1, -1):
            wide_in[t, d] = remote(sets[t][0], sets[t][d % 8], Z, d)

    def wide_arrival(t, h):
        wide_in[t, h].wait_recv()
        d = 1 if h > 0 else -1
        limit = reach[t][0] if h > 0 else reach[t][1]
        if abs(h) < limit:
            wide_in[t, h + d] = remote(sets[t][h % 8], sets[t][(h + d) % 8], Z, d)

    last_in = []

    def pack(t, g):
        a, b, c = KINDS[t]
        n = SIZES[a]
        source = sets[t][g]
        target = packs[t]
        fixed = lax.rem(me[b] - g + SIZES[b], SIZES[b])

        def one(j, carry):
            there = lax.rem(me[a] - j + n, n)
            owner = me[c] * STRIDES[c] + fixed * STRIDES[b] + there * STRIDES[a]
            for k in range(4):
                slot = 0 if k == 0 else (k if c == X else 3 + k)
                for s in range(2):
                    index = jnp.clip(lists_s[slot, s, owner], 0, NB - 1)
                    target[k, g, there, s] = source[j, index]
            return carry

        lax.fori_loop(0, n, one, 0)
        where = [None, None, None]
        where[c] = me[c]
        where[b] = fixed
        where[a] = slice(None)
        spot = pulled.at[
            where[0], where[1], where[2], :, pl.ds(SLICE * t, SLICE), :
        ]
        for k in (1, 3, 2):
            last_in.append(remote(target.at[k, g], spot, c, k))
        local(target.at[0, g], spot)

    half_forward_first(2)
    half_forward_first(3)
    for h in (1, -1):
        for t in (0, 1):
            z_arrival(t, h)
    wide_start(2)
    wide_start(3)
    half_forward(0, 0)
    half_forward(1, 0)
    for copy in list_in:
        copy.wait_recv()
    fetch = local(lists_v, lists_s)
    fetch.wait()
    local_copies.remove(fetch)
    pack(2, 0)
    pack(3, 0)
    for s in (2, 3):
        for h in (s, -s):
            for t in (0, 1):
                z_arrival(t, h)
        for h in (s - 1, 1 - s):
            for t in (0, 1):
                half_forward(t, h)
    z_arrival(0, -4)
    z_arrival(1, 4)
    for h in (3, -3):
        for t in (0, 1):
            half_forward(t, h)
    wide_arrival(2, 1)
    wide_arrival(3, 1)
    wide_arrival(2, -1)
    wide_arrival(3, -1)
    half_forward(0, -4)
    half_forward(1, 4)
    for t in (0, 1):
        pack(t, 0)
    for t in (0, 1):
        pack(t, 1)
        pack(t, 3)
    for t in (0, 1):
        for h in (0, 1, -1, 2, -2, 3, -3, (-4, 4)[t]):
            for copy in mid_in[t, 2, h]:
                copy.wait_recv()
        pack(t, 2)
    for g in (1, 7):
        pack(2, g)
        pack(3, g)
    for s in (2, 3):
        for h in (s, -s):
            for t in (2, 3):
                wide_arrival(t, h)
                pack(t, h % 8)
    wide_arrival(2, 4)
    wide_arrival(3, -4)
    pack(2, 4)
    pack(3, 4)

    for copy in last_in:
        copy.wait_recv()
    for copy in local_copies:
        copy.wait()
    for copy in remote_copies:
        copy.wait_send()


def pull_blocks(blocks, plist):
    chunk8 = pltpu.VMEM((8, NB, SLICE, HALF), jnp.bfloat16)
    chunk4 = pltpu.VMEM((4, NB, SLICE, HALF), jnp.bfloat16)
    return pl.pallas_call(
        pull_kernel,
        out_shape=jax.ShapeDtypeStruct((4, 4, 8, 2, BLK, HALF), jnp.bfloat16),
        in_specs=[pl.BlockSpec(memory_space=pltpu.VMEM)] * 2,
        out_specs=pl.BlockSpec(memory_space=pl.ANY),
        scratch_shapes=[chunk8] * 8
        + [chunk4] * 16
        + [pltpu.VMEM((4, 4, 8, 2, SLICE, HALF), jnp.bfloat16)] * 2
        + [pltpu.VMEM((4, 8, 4, 2, SLICE, HALF), jnp.bfloat16)] * 2
        + [
            pltpu.VMEM((7, 2, 128), jnp.int32),
            pltpu.SMEM((7, 2, 128), jnp.int32),
            pltpu.SemaphoreType.DMA((192,)),
            pltpu.SemaphoreType.DMA((192,)),
            pltpu.SemaphoreType.DMA((32,)),
        ],
        compiler_params=pltpu.CompilerParams(
            collective_id=0, has_side_effects=True, vmem_limit_bytes=48 << 20
        ),
        name="pull_blocks",
    )(blocks, plist)


OWNERS_STEP = 8
STEPS = 128 // OWNERS_STEP
LOCAL_STEP = 64 // STEPS


def sum_kernel(
    plist, rdst, lsrc, ldst, pulled, rtiles, ltiles, hist, mine, following, acc
):
    i = pl.program_id(0)

    @pl.when(i == 0)
    def _():
        acc[...] = jnp.zeros_like(acc)

    terms = []
    for j in range(OWNERS_STEP):
        for c in range(2):
            o = i * OWNERS_STEP + j
            row = jnp.where(plist[c, o] >= 0, rdst[c, o], 2 * NB)
            terms.append(
                (
                    row,
                    jnp.dot(
                        rtiles[j, c], pulled[j, c], preferred_element_type=jnp.float32
                    ),
                )
            )
    for j in range(LOCAL_STEP):
        k = i * LOCAL_STEP + j
        terms.append(
            (
                ldst[0, k],
                jnp.dot(ltiles[j], hist[lsrc[0, k]], preferred_element_type=jnp.float32),
            )
        )
    for row, value in terms:
        acc[row] += value

    @pl.when(i == STEPS - 1)
    def _():
        mine[...] = acc[0:NB]
        following[...] = acc[NB : 2 * NB].astype(jnp.bfloat16)


def sum_tiles(plist, rdst, lsrc, ldst, pulled, rtiles, ltiles, blocks):
    pair = pl.BlockSpec((OWNERS_STEP, 2, BLK, BLK), lambda i, *_: (i, 0, 0, 0))
    return pl.pallas_call(
        sum_kernel,
        out_shape=(
            jax.ShapeDtypeStruct((NB, BLK, HALF), jnp.float32),
            jax.ShapeDtypeStruct((NB, BLK, HALF), jnp.bfloat16),
        ),
        grid_spec=pltpu.PrefetchScalarGridSpec(
            num_scalar_prefetch=4,
            grid=(STEPS,),
            in_specs=[
                pair,
                pair,
                pl.BlockSpec((LOCAL_STEP, BLK, BLK), lambda i, *_: (i, 0, 0)),
                pl.BlockSpec((NB, BLK, HALF), lambda i, *_: (0, 0, 0)),
            ],
            out_specs=[
                pl.BlockSpec((NB, BLK, HALF), lambda i, *_: (0, 0, 0)),
                pl.BlockSpec((NB, BLK, HALF), lambda i, *_: (0, 0, 0)),
            ],
            scratch_shapes=[pltpu.VMEM((2 * NB + 1, BLK, HALF), jnp.float32)],
        ),
        name="sum_tiles",
    )(plist, rdst, lsrc, ldst, pulled, rtiles, ltiles, blocks)


PIECE = 40
ROOT = 0.7978845608028654
CUBIC = 0.044715


def layer_kernel(
    mine,
    following,
    weight,
    bias,
    cotangent,
    new_rows,
    grad_weight,
    grad_bias,
    coming,
    agg,
    other,
    terms,
    z_part,
    plane,
    final,
    send_sems,
    recv_sems,
):
    me, f = coords()
    p = lax.axis_index("dom")
    used = [0]
    copies = []

    def remote(src, dst, dom, feat):
        i = used[0]
        used[0] += 1
        copy = pltpu.make_async_remote_copy(
            src_ref=src,
            dst_ref=dst,
            send_sem=send_sems.at[i],
            recv_sem=recv_sems.at[i],
            device_id=(dom, feat),
            device_id_type=MESH,
        )
        copy.start()
        copies.append(copy)
        return copy

    up = lax.rem(p + 1, 128)
    down = lax.rem(p + 127, 128)
    column = [moved(me, Z, k) for k in range(1, 8)]
    flat = [
        lax.rem(me[0] + i, 4) * 32 + lax.rem(me[1] + j, 4) * 8 + me[2]
        for i in range(4)
        for j in range(4)
        if i or j
    ]
    barrier = pltpu.get_barrier_semaphore()
    greeted = [(up, f), (down, f), (p, 1 - f)] + [(d, f) for d in column + flat]
    for d in greeted:
        pl.semaphore_signal(barrier, inc=1, device_id=d, device_id_type=MESH)
    pl.semaphore_wait(barrier, len(greeted))

    shifts = [remote(following.at[t], coming.at[t], up, f) for t in range(NB)]
    swaps = []
    for t in range(NB):
        shifts[t].wait_recv()
        agg[t] = (mine[t] + coming[t].astype(jnp.float32)).astype(jnp.bfloat16)
        swaps.append(remote(agg.at[t], other.at[t], p, 1 - f))
    w_mine = weight[pl.ds(pl.multiple_of(f * HALF, HALF), HALF), :]
    w_other = weight[pl.ds(pl.multiple_of((1 - f) * HALF, HALF), HALF), :]
    b = bias[...]
    g_mine = jnp.zeros((HALF, HALF), jnp.float32)
    g_other = jnp.zeros((HALF, HALF), jnp.float32)
    g_bias = jnp.zeros((8, HALF), jnp.float32)
    for t in range(NB):
        swaps[t].wait_recv()
        a0 = agg[t]
        a1 = other[t]
        v = (
            jnp.dot(a0, w_mine, preferred_element_type=jnp.float32)
            + jnp.dot(a1, w_other, preferred_element_type=jnp.float32)
            + b
        )
        v2 = v * v
        th = jnp.tanh(ROOT * (v + CUBIC * (v2 * v)))
        half = 0.5 * (1.0 + th)
        rows = slice(BLK * t, BLK * (t + 1))
        new_rows[rows, :] = (v * half).astype(jnp.bfloat16)
        slope = half + (0.5 * ROOT) * v * (1.0 - th * th) * (1.0 + (3.0 * CUBIC) * v2)
        gp = (cotangent[rows, :].astype(jnp.float32) * slope).astype(jnp.bfloat16)
        dims = (((0,), (0,)), ((), ()))
        g_mine += lax.dot_general(a0, gp, dims, preferred_element_type=jnp.float32)
        g_other += lax.dot_general(a1, gp, dims, preferred_element_type=jnp.float32)
        g_bias += jnp.sum(gp.astype(jnp.float32).reshape(16, 8, HALF), axis=0)
    terms[pl.ds(f * 4, 4), 0:32, :] = g_mine.reshape(4, 32, HALF)
    terms[pl.ds((1 - f) * 4, 4), 0:32, :] = g_other.reshape(4, 32, HALF)
    terms[:, 32:40, :] = jnp.zeros((8, 8, HALF), jnp.float32)
    terms[0, 32:40, :] = g_bias

    ins = []
    for k in range(1, 8):
        there = lax.rem(me[2] + k, 8)
        ins.append(remote(terms.at[there], z_part.at[k - 1], column[k - 1], f))
    total = terms[me[2]]
    for k in range(7):
        ins[k].wait_recv()
        total = total + z_part[k]
    spot = me[0] * 4 + me[1]
    plane[spot] = total
    ins = [remote(plane.at[spot], plane.at[spot], d, f) for d in flat]
    for copy in ins:
        copy.wait_recv()
    total = plane[0]
    for k in range(1, 16):
        total = total + plane[k]
    final[me[2]] = total
    ins = [remote(final.at[me[2]], final.at[me[2]], d, f) for d in column]
    for copy in ins:
        copy.wait_recv()
    for k in range(8):
        grad_weight[32 * k : 32 * (k + 1), :] = final[k, 0:32, :]
    grad_bias[...] = jnp.sum(final[0, 32:40, :], axis=0, keepdims=True)
    for copy in copies:
        copy.wait_send()


def layer(mine, following, weight, bias, cotangent):
    vm = pl.BlockSpec(memory_space=pltpu.VMEM)
    return pl.pallas_call(
        layer_kernel,
        out_shape=(
            jax.ShapeDtypeStruct((NB * BLK, HALF), jnp.bfloat16),
            jax.ShapeDtypeStruct((2 * HALF, HALF), jnp.float32),
            jax.ShapeDtypeStruct((1, HALF), jnp.float32),
        ),
        in_specs=[vm] * 5,
        out_specs=(vm, vm, vm),
        scratch_shapes=[
            pltpu.VMEM((NB, BLK, HALF), jnp.bfloat16),
            pltpu.VMEM((NB, BLK, HALF), jnp.bfloat16),
            pltpu.VMEM((NB, BLK, HALF), jnp.bfloat16),
            pltpu.VMEM((8, PIECE, HALF), jnp.float32),
            pltpu.VMEM((7, PIECE, HALF), jnp.float32),
            pltpu.VMEM((16, PIECE, HALF), jnp.float32),
            pltpu.VMEM((8, PIECE, HALF), jnp.float32),
            pltpu.SemaphoreType.DMA((48,)),
            pltpu.SemaphoreType.DMA((48,)),
        ],
        compiler_params=pltpu.CompilerParams(
            collective_id=1, has_side_effects=True, vmem_limit_bytes=32 << 20
        ),
        name="layer",
    )(mine, following, weight, bias, cotangent)


def per_device(
    history,
    pull_list,
    remote_tiles,
    remote_dst,
    local_tiles,
    local_src,
    local_dst,
    weight,
    bias,
    cotangent,
):
    blocks = history.reshape(NB, BLK, HALF)
    plist = pull_list[0].T
    pulled = pull_blocks(blocks, plist)
    mine, following = sum_tiles(
        plist,
        remote_dst[0].T,
        local_src,
        local_dst,
        pulled.reshape(128, 2, BLK, HALF),
        remote_tiles[0],
        local_tiles,
        blocks,
    )
    new_rows, grad_weight, grad_bias = layer(
        mine, following, weight, bias.reshape(1, HALF), cotangent
    )
    return new_rows, grad_weight, grad_bias.reshape(HALF)


def solution(mesh):
    placed = (
        P("dom", "feat"),
        P("dom", None, None),
        P("dom", None, None, None, None),
        P("dom", None, None),
        P("dom", None, None),
        P("dom", None),
        P("dom", None),
        P(None, "feat"),
        P("feat"),
        P("dom", "feat"),
    )
    return jax.shard_map(
        per_device,
        mesh=mesh,
        in_specs=placed,
        out_specs=(P("dom", "feat"), P(None, "feat"), P("feat")),
        check_vma=False,
    )
```

time: 686 us -> 141 us (0.21)
  the two profiles are of different devices: /device:TPU:32 before, /device:TPU:24 now
where the time goes in v1:
time: 141 us; the launch traced here: 140 us
  Pallas kernels  134 us (95%)
  local copies, waits for them, and re-layouts  5.5 us (4%)
    pallas_call x1, Pallas kernels, pull_blocks(): pl.pallas_call(pull_kernel, out_shape=jax.ShapeDtypeStruct((4, 4, 8, 2, B...  85.4 us
    pallas_call x1, Pallas kernels, layer(): pl.pallas_call(layer_kernel, out_shape=(jax.ShapeDtypeStruct((NB * BLK, H...  33.1 us
    pallas_call x1, Pallas kernels, sum_tiles(): pl.pallas_call(sum_kernel, out_shape=(jax.ShapeDtypeStruct((NB, BLK, HALF...  15.6 us
    unnamed x17, local copies, waits for them, and re-layouts  5.5 us

profile of v1, /device:TPU:24, one launch (start us, length us, event | category | flops | bytes accessed | tf_op | source)
XLA Modules:
  0.0 140.4 jit_solution(13056746813237340630)
XLA Ops:
  0.6 0.0 copy-start
  0.6 0.9 copy-done
  1.6 0.0 copy-start.5
  1.6 0.7 copy-done.5
  2.3 85.4 %pull_blocks.1 = bf16[4,4,8,2,128,128]{5,4,3,2,1,0:T(8,128)(2,1)} custom-call(bf16[8,128,128]{2,1,0:T(8,128)(2,1)S(1)} %bitcast.12, s32[2,128]{1,0:T(2,128)S(1)} %bitcast.14), custom_call_target="tpu_custom_call" | custom-call | tf_op jit(solution)/shard_map/pull_blocks/pallas_call | solution.py:244
  87.7 0.0 copy-start.2
  87.7 0.0 copy-start.4
  87.7 0.0 copy-start.6
  87.7 15.6 %sum_tiles.1 = (f32[8,128,128]{2,1,0:T(8,128)}, bf16[8,128,128]{2,1,0:T(8,128)(2,1)}) custom-call(s32[2,128]{1,0:T(2,128)} %bitcast.13, s32[2,128]{1,0:T(2,128)} %bitcast.19, s32[1,64]{1,0:T(1,128)} %lsrc.1, s32[1,64]{1,0:T(1,128)} %ldst.1, bf16[128,2,128,128]{3,2,1,0:T(8,128)(2,1)} %bitcast.17, bf16[128,2,128,128]{3,2,1,0:T(8,128)(2,1)} %bitcast.18, ...), custom_call_target="tpu_custom_call" | custom-call | tf_op jit(solution)/shard_map/sum_tiles/pallas_call | solution.py:313
  103.4 0.0 copy-done.2
  103.4 0.0 copy-done.4
  103.4 0.0 copy-done.6
  103.4 0.0 copy-start.1
  103.4 1.0 copy-done.1
  104.5 0.0 copy-start.3
  104.5 0.9 copy-done.3
  105.4 33.1 %layer.1 = (bf16[1024,128]{1,0:T(8,128)(2,1)S(1)}, f32[256,128]{1,0:T(8,128)S(1)}, f32[1,128]{1,0:T(1,128)S(1)}) custom-call(f32[8,128,128]{2,1,0:T(8,128)S(1)} %copy-done.1, bf16[8,128,128]{2,1,0:T(8,128)(2,1)S(1)} %copy-done.3, bf16[256,128]{1,0:T(8,128)(2,1)S(1)} %copy-done.4, f32[1,128]{1,0:T(1,128)S(1)} %bitcast.15, bf16[1024,128]{1,0:T(8,128)(2,1)S(1)} %copy-done.2), custom_call_target="tpu_custom_call" | custom-call | tf_op jit(solution)/shard_map/layer/pallas_call | solution.py:463
  138.5 0.7 copy.16
  139.2 0.7 copy.17
  139.9 0.5 copy.18
Async XLA Ops:
  0.6 1.0 copy-start
  1.6 0.7 copy-start.5
  87.7 15.7 %copy-start.2 = (bf16[1024,128]{1,0:T(8,128)(2,1)S(1)}, bf16[1024,128]{1,0:T(8,128)(2,1)}, u32[]{:S(2)}) copy-start(bf16[1024,128]{1,0:T(8,128)(2,1)} %cotangent.1) | copy-start | bytes 786436
  87.7 15.7 %copy-start.4 = (bf16[256,128]{1,0:T(8,128)(2,1)S(1)}, bf16[256,128]{1,0:T(8,128)(2,1)}, u32[]{:S(2)}) copy-start(bf16[256,128]{1,0:T(8,128)(2,1)} %weight.1) | copy-start | bytes 196612
  87.7 15.7 %copy-start.6 = (f32[128]{0:T(128)S(1)}, f32[128]{0:T(128)}, u32[]{:S(2)}) copy-start(f32[128]{0:T(128)} %param.18) | copy-start | bytes 1540
  103.4 1.0 copy-start.1
  104.5 0.9 copy-start.3

commit v2 on v0

v2 whole, which is shorter than its diff:
```python
import functools

import jax
import jax.numpy as jnp
from jax import lax
from jax.sharding import PartitionSpec as P
from jax.experimental import pallas as pl
from jax.experimental.pallas import tpu as pltpu

MESH = pl.DeviceIdType.MESH
X, Y, Z = 0, 1, 2
SIZES = (4, 4, 8)
STRIDES = (32, 8, 1)
NB = 8
BLK = 128
HALF = 128
SLICE = 32
KINDS = ((Z, Y, X), (Z, X, Y), (Y, Z, X), (X, Z, Y))


def coords():
    p = lax.axis_index("dom")
    return (p // 32, lax.rem(p // 8, 4), lax.rem(p, 8)), lax.axis_index("feat")


def group_rank(h):
    return jnp.where(h == 0, 0, jnp.where(h <= 4, 2 * h - 1, 2 * (8 - h)))


def moved(me, axis, offset):
    n = SIZES[axis]
    there = list(me)
    there[axis] = lax.rem(me[axis] + (offset % n), n)
    return there[0] * 32 + there[1] * 8 + there[2]


PIECE = 24
ROOT = 0.7978845608028654
CUBIC = 0.044715
TILES = 320
LOCAL = 64


def step_kernel(
    history,
    table,
    rtiles,
    ltiles,
    cotangent,
    weight,
    bias,
    new_rows,
    grad_weight,
    grad_bias,
    *scratch,
):
    sets = [scratch[0:4], scratch[4:8], scratch[8:16], scratch[16:24]]
    packs = scratch[24:28]
    (
        lists_v,
        lists_s,
        hist,
        rt,
        lt,
        cot,
        pulled,
        sums,
        following,
        coming,
        agg,
        other,
        terms,
        part,
        column_sums,
        final,
        send_sems,
        recv_sems,
        local_sems,
    ) = scratch[28:]
    me, f = coords()
    p = lax.axis_index("dom")
    used = [0, 0]
    remote_copies = []

    def send(src, dst, dom, feat):
        i = used[0]
        used[0] += 1
        copy = pltpu.make_async_remote_copy(
            src_ref=src,
            dst_ref=dst,
            send_sem=send_sems.at[i],
            recv_sem=recv_sems.at[i],
            device_id=(dom, feat),
            device_id_type=MESH,
        )
        copy.start()
        remote_copies.append(copy)
        return copy

    def remote(src, dst, axis, offset):
        return send(src, dst, moved(me, axis, offset), f)

    def local(src, dst):
        i = used[1]
        used[1] += 1
        copy = pltpu.make_async_copy(src, dst, local_sems.at[i])
        copy.start()
        return copy

    def own(t):
        return hist.at[:, pl.ds(SLICE * t, SLICE), :]

    load_hist = local(history, hist)
    up = lax.rem(p + 1, 128)
    down = lax.rem(p + 127, 128)
    column = [moved(me, Z, k) for k in range(1, 8)]
    flat = [
        lax.rem(me[0] + i, 4) * 32 + lax.rem(me[1] + j, 4) * 8 + me[2]
        for i in range(4)
        for j in range(4)
        if i or j
    ]
    barrier = pltpu.get_barrier_semaphore()
    greeted = [(up, f), (down, f), (p, 1 - f)] + [(d, f) for d in column + flat]
    for d in greeted:
        pl.semaphore_signal(barrier, inc=1, device_id=d, device_id_type=MESH)
    load_rt = local(rtiles, rt)
    load_lt = local(ltiles, lt)
    load_cot = local(cotangent, cot)
    sums[TILES] = jnp.zeros((BLK, HALF), jnp.float32)
    load_hist.wait()
    pl.semaphore_wait(barrier, len(greeted))

    z_in = {}
    mid_in = {}
    wide_in = {}
    last_in = {}
    list_in = []
    reach = {0: (3, 4), 1: (4, 3), 2: (4, 3), 3: (3, 4)}

    def z_start(t):
        for d in (1, -1):
            z_in[t, d] = remote(own(t), sets[t][0].at[d % 8], Z, d)

    def first_start(t):
        for d in (1, -1):
            mid_in[t, d] = remote(own(t), sets[t][0].at[d % 4], KINDS[t][0], d)

    def mid_start(t):
        for d in (1, -1):
            mid_in[t, d, 0] = remote(own(t), sets[t][d % 4].at[0], KINDS[t][1], d)

    def lists_start():
        for i, axis in enumerate((X, Y)):
            for k in (1, 2, 3):
                list_in.append(remote(table, lists_v.at[3 * i + k], axis, -k))

    def lists_end():
        for copy in list_in:
            copy.wait_recv()
        local(lists_v, lists_s).wait()

    def half_forward_first(t):
        a = KINDS[t][0]
        ring = sets[t][0]
        mid_in[t, 1].wait_recv()
        u = remote(ring.at[1, pl.ds(0, 4)], ring.at[2, pl.ds(0, 4)], a, 1)
        mid_in[t, -1].wait_recv()
        v = remote(ring.at[3, pl.ds(4, 4)], ring.at[2, pl.ds(4, 4)], a, -1)
        mid_in[t, 2] = (u, v)

    def first_end(t):
        for copy in mid_in[t, 2]:
            copy.wait_recv()

    def z_arrival(t, h):
        z_in[t, h].wait_recv()
        d = 1 if h > 0 else -1
        limit = reach[t][0] if h > 0 else reach[t][1]
        here = sets[t][0].at[h % 8]
        if abs(h) < limit:
            z_in[t, h + d] = remote(here, sets[t][0].at[(h + d) % 8], Z, d)
        for e in (1, -1):
            mid_in[t, e, h] = remote(here, sets[t][e % 4].at[h % 8], KINDS[t][1], e)

    def half_forward(t, h):
        b = KINDS[t][1]
        s = h % 8
        mid_in[t, 1, h].wait_recv()
        u = remote(sets[t][1].at[s, pl.ds(0, 4)], sets[t][2].at[s, pl.ds(0, 4)], b, 1)
        mid_in[t, -1, h].wait_recv()
        v = remote(sets[t][3].at[s, pl.ds(4, 4)], sets[t][2].at[s, pl.ds(4, 4)], b, -1)
        mid_in[t, 2, h] = (u, v)

    def half_end(t):
        for h in (0, 1, -1, 2, -2, 3, -3, (-4, 4)[t]):
            for copy in mid_in[t, 2, h]:
                copy.wait_recv()

    def wide_start(t, q):
        source = own(t) if q == 0 else sets[t][0].at[q]
        for d in (1, -1):
            wide_in[t, d, q] = remote(source, sets[t][d % 8].at[q], Z, d)

    def wide_arrival(t, h, q):
        if (t, h, q) not in wide_in:
            return
        wide_in[t, h, q].wait_recv()
        d = 1 if h > 0 else -1
        limit = reach[t][0] if h > 0 else reach[t][1]
        if abs(h) < limit:
            wide_in[t, h + d, q] = remote(
                sets[t][h % 8].at[q], sets[t][(h + d) % 8].at[q], Z, d
            )

    def pack(t, g):
        a, b, c = KINDS[t]
        n = SIZES[a]
        source = sets[t][g]
        target = packs[t]
        fixed = lax.rem(me[b] - g + SIZES[b], SIZES[b])
        rows = pl.ds(SLICE * t, SLICE)

        def spot(there, *rest):
            where = [None, None, None]
            where[c] = me[c]
            where[b] = fixed
            where[a] = there
            return (where[0], where[1], where[2]) + rest

        def one(j, carry):
            there = lax.rem(me[a] - j + n, n)
            owner = me[c] * STRIDES[c] + fixed * STRIDES[b] + there * STRIDES[a]
            for k in range(4):
                slot = 0 if k == 0 else (k if c == X else 3 + k)
                for s in range(2):
                    index = jnp.clip(lists_s[slot, s, owner], 0, NB - 1)
                    value = source[j, index]
                    if k == 0:
                        pulled[spot(there, s, rows, slice(None))] = value
                    else:
                        target[k - 1, g, there, s] = value
            return carry

        lax.fori_loop(0, n, one, 0)
        to = pulled.at[spot(slice(None), slice(None), rows, slice(None))]
        last_in[t, g] = [remote(target.at[k - 1, g], to, c, k) for k in (1, 3, 2)]

    def arrived(t, g):
        for copy in last_in[t, g]:
            copy.wait_recv()

    def local_tiles(start, stop):
        def eight(i, carry):
            values = []
            for j in range(8):
                k = i * 8 + j
                values.append(
                    jnp.dot(
                        lt[k], hist[lists_s[0, 5, k]], preferred_element_type=jnp.float32
                    )
                )
            for j in range(8):
                k = i * 8 + j
                sums[k] = sums[lists_s[0, 4, k]] + values[j]
            return carry

        lax.fori_loop(start, stop, eight, 0)

    order = (0, 1, 7, 2, 6, 3, 5, 4)

    def remote_tiles(g):
        first = LOCAL + 32 * order.index(g)
        z = lax.rem(me[2] - g + 8, 8)

        def eight(i, carry):
            values = []
            for j in range(4):
                o = i * 32 + j * 8 + z
                for c in range(2):
                    values.append(
                        jnp.dot(
                            rt[o, c], pulled[i, j, z, c], preferred_element_type=jnp.float32
                        )
                    )
            for j in range(4):
                o = i * 32 + j * 8 + z
                for c in range(2):
                    sums[first + i * 8 + j * 2 + c] = (
                        sums[lists_s[0, 2 + c, o]] + values[2 * j + c]
                    )
            return carry

        lax.fori_loop(0, 4, eight, 0)


    z_start(0)
    z_start(1)
    first_start(2)
    first_start(3)
    lists_start()
    mid_start(0)
    mid_start(1)
    for t in range(4):
        sets[t][0][0] = hist[:, SLICE * t : SLICE * (t + 1), :]
    lists_v[0] = table[...]
    wide_start(2, 0)
    wide_start(3, 0)
    half_forward_first(2)
    half_forward_first(3)
    for h in (1, -1):
        for t in (0, 1):
            z_arrival(t, h)
    half_forward(0, 0)
    half_forward(1, 0)
    lists_end()
    first_end(2)
    first_end(3)
    pack(2, 0)
    pack(3, 0)
    wide_start(2, 1)
    wide_start(3, 1)
    for h in (2, -2):
        for t in (0, 1):
            z_arrival(t, h)
    for h in (1, -1):
        for t in (0, 1):
            half_forward(t, h)
    wide_start(2, 3)
    wide_start(3, 3)
    for h in (3, -3):
        for t in (0, 1):
            z_arrival(t, h)
    wide_start(2, 2)
    wide_start(3, 2)
    for h in (1, -1):
        for t in (2, 3):
            wide_arrival(t, h, 0)
    for h in (2, -2):
        for t in (0, 1):
            half_forward(t, h)
    for h in (1, -1):
        for t in (2, 3):
            wide_arrival(t, h, 1)
    z_arrival(0, -4)
    z_arrival(1, 4)
    for h in (3, -3):
        for t in (0, 1):
            half_forward(t, h)
    pack(0, 0)
    pack(1, 0)
    for h in (1, -1):
        for t in (2, 3):
            wide_arrival(t, h, 3)
    half_forward(0, -4)
    half_forward(1, 4)
    for g in (1, 3):
        pack(0, g)
        pack(1, g)
    for h in (1, -1):
        for t in (2, 3):
            wide_arrival(t, h, 2)
    for g in (1, 7):
        pack(2, g)
        pack(3, g)
    for t in (0, 1):
        half_end(t)
        pack(t, 2)
    load_lt.wait()
    for s in (2, 3, 4):
        for i, q in enumerate((0, 1, 3, 2)):
            for h in (s, -s):
                for t in (2, 3):
                    wide_arrival(t, h, q)
            if s == 2:
                local_tiles(2 * i, 2 * i + 2)
        for h in (s, -s):
            for t in (2, 3):
                if (t, h, 0) in wide_in:
                    pack(t, h % 8)
    load_rt.wait()
    for t in (0, 1):
        for g in (0, 1, 3, 2):
            arrived(t, g)
    for g in order:
        arrived(2, g)
        arrived(3, g)
        remote_tiles(g)

    load_cot.wait()
    shifts = []
    for t in range(NB):
        following[t] = sums[lists_s[0, 4, 64 + NB + t]].astype(jnp.bfloat16)
        shifts.append(send(following.at[t], coming.at[t], up, f))
    swaps = []
    for t in range(NB):
        mine = sums[lists_s[0, 4, 64 + t]]
        shifts[t].wait_recv()
        agg[t] = (mine + coming[t].astype(jnp.float32)).astype(jnp.bfloat16)
        swaps.append(send(agg.at[t], other.at[t], p, 1 - f))
    w_mine = weight[pl.ds(pl.multiple_of(f * HALF, HALF), HALF), :]
    w_other = weight[pl.ds(pl.multiple_of((1 - f) * HALF, HALF), HALF), :]
    b = bias[...]
    g_mine = jnp.zeros((HALF, HALF), jnp.float32)
    g_other = jnp.zeros((HALF, HALF), jnp.float32)
    g_bias = jnp.zeros((8, HALF), jnp.float32)
    for t in range(NB):
        swaps[t].wait_recv()
        a0 = agg[t]
        a1 = other[t]
        v = (
            jnp.dot(a0, w_mine, preferred_element_type=jnp.float32)
            + jnp.dot(a1, w_other, preferred_element_type=jnp.float32)
            + b
        )
        v2 = v * v
        th = jnp.tanh(ROOT * (v + CUBIC * (v2 * v)))
        half = 0.5 * (1.0 + th)
        rows = slice(BLK * t, BLK * (t + 1))
        new_rows[rows, :] = (v * half).astype(jnp.bfloat16)
        slope = half + (0.5 * ROOT) * v * (1.0 - th * th) * (1.0 + (3.0 * CUBIC) * v2)
        gp = (cot[rows, :].astype(jnp.float32) * slope).astype(jnp.bfloat16)
        dims = (((0,), (0,)), ((), ()))
        g_mine += lax.dot_general(a0, gp, dims, preferred_element_type=jnp.float32)
        g_other += lax.dot_general(a1, gp, dims, preferred_element_type=jnp.float32)
        g_bias += jnp.sum(gp.astype(jnp.float32).reshape(16, 8, HALF), axis=0)
    terms[pl.ds(f * 8, 8), 0:16, :] = g_mine.reshape(8, 16, HALF)
    terms[pl.ds((1 - f) * 8, 8), 0:16, :] = g_other.reshape(8, 16, HALF)
    terms[:, 16:24, :] = jnp.zeros((16, 8, HALF), jnp.float32)
    terms[0, 16:24, :] = g_bias

    spot = me[0] * 4 + me[1]
    ins = [send(terms.at[d // 8], part.at[i], d, f) for i, d in enumerate(flat)]
    total = terms[spot]
    for i in range(15):
        ins[i].wait_recv()
        total = total + part[i]
    column_sums[me[2]] = total
    ins = [send(column_sums.at[me[2]], column_sums.at[me[2]], d, f) for d in column]
    for copy in ins:
        copy.wait_recv()
    total = column_sums[0]
    for k in range(1, 8):
        total = total + column_sums[k]
    final[spot] = total
    ins = [send(final.at[spot], final.at[spot], d, f) for d in flat]
    for copy in ins:
        copy.wait_recv()
    for k in range(16):
        grad_weight[16 * k : 16 * (k + 1), :] = final[k, 0:16, :]
    grad_bias[...] = jnp.sum(final[0, 16:24, :], axis=0, keepdims=True)
    for copy in remote_copies:
        copy.wait_send()


def step(blocks, table, rtiles, ltiles, cotangent, weight, bias):
    vm = pl.BlockSpec(memory_space=pltpu.VMEM)
    hbm = pl.BlockSpec(memory_space=pl.ANY)
    bf16 = jnp.bfloat16
    f32 = jnp.float32
    return pl.pallas_call(
        step_kernel,
        out_shape=(
            jax.ShapeDtypeStruct((NB * BLK, HALF), bf16),
            jax.ShapeDtypeStruct((2 * HALF, HALF), f32),
            jax.ShapeDtypeStruct((1, HALF), f32),
        ),
        in_specs=[hbm, vm, hbm, hbm, hbm, vm, vm],
        out_specs=(vm, vm, vm),
        scratch_shapes=[pltpu.VMEM((8, NB, SLICE, HALF), bf16)] * 8
        + [pltpu.VMEM((4, NB, SLICE, HALF), bf16)] * 16
        + [pltpu.VMEM((3, 4, 8, 2, SLICE, HALF), bf16)] * 2
        + [pltpu.VMEM((3, 8, 4, 2, SLICE, HALF), bf16)] * 2
        + [
            pltpu.VMEM((7, 8, 128), jnp.int32),
            pltpu.SMEM((7, 8, 128), jnp.int32),
            pltpu.VMEM((NB, BLK, HALF), bf16),
            pltpu.VMEM((128, 2, BLK, BLK), bf16),
            pltpu.VMEM((LOCAL, BLK, BLK), bf16),
            pltpu.VMEM((NB * BLK, HALF), bf16),
            pltpu.VMEM((4, 4, 8, 2, BLK, HALF), bf16),
            pltpu.VMEM((TILES + 1, BLK, HALF), f32),
            pltpu.VMEM((NB, BLK, HALF), bf16),
            pltpu.VMEM((NB, BLK, HALF), bf16),
            pltpu.VMEM((NB, BLK, HALF), bf16),
            pltpu.VMEM((NB, BLK, HALF), bf16),
            pltpu.VMEM((16, PIECE, HALF), f32),
            pltpu.VMEM((15, PIECE, HALF), f32),
            pltpu.VMEM((8, PIECE, HALF), f32),
            pltpu.VMEM((16, PIECE, HALF), f32),
            pltpu.SemaphoreType.DMA((320,)),
            pltpu.SemaphoreType.DMA((320,)),
            pltpu.SemaphoreType.DMA((8,)),
        ],
        compiler_params=pltpu.CompilerParams(
            collective_id=0, has_side_effects=True, vmem_limit_bytes=67043328
        ),
        name="step",
    )(blocks, table, rtiles, ltiles, cotangent, weight, bias)


def index_table(plist, remote_dst, local_src, local_dst):
    mz = lax.rem(lax.axis_index("dom"), 8)
    i = jnp.arange(256, dtype=jnp.int32)
    o = i // 2
    h = lax.rem(mz - lax.rem(o, 8) + 8, 8)
    key = LOCAL + group_rank(h) * 32 + (o // 32) * 8 + lax.rem(o // 8, 4) * 2 + lax.rem(i, 2)
    near = jnp.arange(LOCAL, dtype=jnp.int32)
    dst = jnp.where(plist.reshape(-1) >= 0, remote_dst.reshape(-1), -1)
    dst = jnp.concatenate([local_dst.reshape(-1), dst])
    keys = jnp.concatenate([near, key])
    want = jnp.concatenate(
        [remote_dst.T.reshape(-1), local_dst.reshape(-1), jnp.arange(16, dtype=jnp.int32)]
    )
    limit = jnp.concatenate(
        [key.reshape(128, 2).T.reshape(-1), near, jnp.full((16,), TILES, jnp.int32)]
    )
    match = (want[:, None] == dst[None, :]) & (keys[None, :] < limit[:, None])
    before = jnp.max(jnp.where(match, keys[None, :], -1), axis=1)
    before = jnp.where(before < 0, TILES, before)
    return jnp.concatenate(
        [
            plist.T.reshape(-1),
            before,
            jnp.zeros((48,), jnp.int32),
            local_src.reshape(-1),
            jnp.zeros((64 + 256,), jnp.int32),
        ]
    ).reshape(8, 128)


def per_device(
    history,
    pull_list,
    remote_tiles,
    remote_dst,
    local_tiles,
    local_src,
    local_dst,
    weight,
    bias,
    cotangent,
):
    table = index_table(pull_list[0], remote_dst[0], local_src, local_dst)
    new_rows, grad_weight, grad_bias = step(
        history.reshape(NB, BLK, HALF),
        table,
        remote_tiles[0],
        local_tiles,
        cotangent,
        weight,
        bias.reshape(1, HALF),
    )
    return new_rows, grad_weight, grad_bias.reshape(HALF)


def solution(mesh):
    placed = (
        P("dom", "feat"),
        P("dom", None, None),
        P("dom", None, None, None, None),
        P("dom", None, None),
        P("dom", None, None),
        P("dom", None),
        P("dom", None),
        P(None, "feat"),
        P("feat"),
        P("dom", "feat"),
    )
    return jax.shard_map(
        per_device,
        mesh=mesh,
        in_specs=placed,
        out_specs=(P("dom", "feat"), P(None, "feat"), P("feat")),
        check_vma=False,
    )
```

time: 686 us -> 119 us (0.17)
  blocking collectives: 374 us -> 0 us
  waiting for transfers between devices: 180 us -> 0 us
  Pallas kernels: 0 us -> 109 us
  matrix products: 51.1 us -> 0 us
  local copies, waits for them, and re-layouts: 50 us -> 6.02 us
  between operations: 14.2 us -> 0.7 us
  starting transfers between devices: 8.32 us -> 0 us
    psum x1 -> x0, blocking collectives: 346 us -> none  [per_device(): grad_weight, grad_bias = lax.psum((weight_term, bias_term), 'dom')]
    all_to_all x1 -> x0, waiting for transfers between devices: 168 us -> none  [per_device(): lax.all_to_all(jnp.where((asked >= 0)[:, :, None, None], picked, jnp.zero...]
    pallas_call x0 -> x1, Pallas kernels: none -> 109 us  [step(): pl.pallas_call(step_kernel, out_shape=(jax.ShapeDtypeStruct((NB * BLK, HA...]
    dot_general x6 -> x0, matrix products: 51.1 us -> none  [the longest x2 26.2 us: select_rows(): return jnp.dot(one_hot, values, precision=lax.Precision.HIGHEST)]
    all_to_all x1 -> x0, blocking collectives: 26 us -> none  [per_device(): lax.all_to_all(requested, 'dom', split_axis=0, concat_axis=0, tiled=True)]
    gather x3 -> x0, local copies, waits for them, and re-layouts: 23.6 us -> none  [the longest x2 21.4 us: per_device(): picked = blocks[clamped]]
    dot_general x2 -> x0, local copies, waits for them, and re-layouts: 23 us -> none  [the longest x1 17.4 us: per_device(): jnp.einsum('ockj,ocjf->ockf', remote_tiles[0], pulled, preferred_element_...]
    ppermute x1 -> x0, waiting for transfers between devices: 11.8 us -> none  [passed_along(): return lax.ppermute(block, axis, route)]
  transfers between devices with their start and end apart: 3 -> 0, of which waited for: 2 -> 0; matrix products, arithmetic and copies ran while one was open for 3% -> 0% of each run, Pallas kernels for 0% -> 0%
where the time goes in v2:
time: 119 us; the launch traced here: 118 us
  Pallas kernels  109 us (92%)
  local copies, waits for them, and re-layouts  6.02 us (5%)
  other arithmetic  2.58 us (2%)
    pallas_call x1, Pallas kernels, step(): pl.pallas_call(step_kernel, out_shape=(jax.ShapeDtypeStruct((NB * BLK, HA...  109 us
    unnamed x3, local copies, waits for them, and re-layouts  4.41 us

profile of v2, /device:TPU:32, one launch (start us, length us, event | category | flops | bytes accessed | tf_op | source)
XLA Modules:
  0.0 118.4 jit_solution(6951015094529573405)
XLA Ops:
  0.7 0.7 compare_select_fusion.13
  1.4 0.8 pad_add_fusion
  2.2 0.1 pad_add_fusion.2
  2.2 0.1 pad_add_fusion.3
  2.3 0.1 copy.14
  2.4 0.1 select_n.67
  2.6 0.7 pad_add_fusion.1
  3.3 0.2 select_reduce_fusion
  3.5 1.3 %concatenate.19 = s32[1024]{0:T(1024)} concatenate(s32[256]{0:T(256)} %bitcast.34, s32[336]{0:T(512)S(1)} %compare_select_fusion, s32[48]{0:T(128)S(1)} %broadcast_in_dim.37, s32[64]{0:T(128)} %bitcast.38, s32[320]{0:T(512)S(1)} %broadcast_in_dim.38), dimensions={0} | concatenate | bytes 8192 | tf_op jit(solution)/shard_map/concatenate | solution.py:521
  4.9 109.1 %step.1 = (bf16[1024,128]{1,0:T(8,128)(2,1)}, f32[256,128]{1,0:T(8,128)}, f32[1,128]{1,0:T(1,128)}) custom-call(bf16[8,128,128]{2,1,0:T(8,128)(2,1)} %bitcast.32, s32[8,128]{1,0:T(8,128)} %bitcast.33, bf16[128,2,128,128]{3,2,1,0:T(8,128)(2,1)} %bitcast.31, bf16[64,128,128]{2,1,0:T(8,128)(2,1)} %ltiles.1, bf16[1024,128]{1,0:T(8,128)(2,1)} %cotangent.1, ...), custom_call_target="tpu_custom_call" | custom-call | tf_op jit(solution)/shard_map/step/pallas_call | solution.py:461
  114.0 1.7 %copy.18 = bf16[1024,128]{1,0:T(8,128)(2,1)} copy(bf16[1024,128]{1,0:T(8,128)(2,1)} %get-tuple-element.14) | data formatting | bytes 524288
  115.7 1.6 %copy.19 = f32[256,128]{1,0:T(8,128)} copy(f32[256,128]{1,0:T(8,128)} %get-tuple-element.15) | data formatting | bytes 262144
  117.2 1.2 copy.20
  (8 shorter events, 0.1 us)

commit v3 on v2

--- a/solution.py
+++ b/solution.py
@@ -39,16 +39,45 @@
 CUBIC = 0.044715
 TILES = 320
 LOCAL = 64
+LAG = 2
+SLOTS = 3
+EVENTS = (
+    ("s", 2, 0), ("z", 0, 1), ("z", 0, -1), ("f", 2, 1), ("f", 2, -1), ("f", 3, 1), ("f", 3, -1),
+    ("z", 1, 1), ("z", 1, -1), ("m", 0, 1, 0), ("m", 0, -1, 0), ("m", 1, 1, 0), ("m", 1, -1, 0),
+    ("w", 2, 1, 0), ("w", 2, -1, 0), ("m", 0, 1, 1), ("m", 0, -1, 1), ("m", 1, 1, 1), ("m", 1, -1, 1),
+    ("p", 3, 0), ("z", 0, 2), ("z", 0, -2), ("m", 0, 1, -1), ("m", 0, -1, -1), ("p", 2, 0), ("m", 1, 1, -1),
+    ("m", 1, -1, -1), ("z", 1, 2), ("z", 1, -2), ("w", 2, 2, 0), ("w", 2, -2, 0), ("z", 0, 3), ("z", 0, -3),
+    ("s", 3, 0), ("z", 1, 3), ("z", 1, -3), ("m", 0, 1, 2), ("m", 0, -1, 2), ("w", 2, 3, 0), ("w", 2, -3, 0),
+    ("s", 2, 1), ("m", 1, 1, 2), ("m", 1, -1, 2), ("m", 0, 1, -2), ("m", 0, -1, -2), ("w", 3, 1, 0),
+    ("z", 0, -4), ("s", 2, 3), ("m", 1, 1, -2), ("m", 1, -1, -2), ("z", 1, 4), ("w", 3, -1, 0),
+    ("m", 0, 1, 3), ("m", 0, -1, 3), ("m", 1, 1, 3), ("m", 1, -1, 3), ("w", 2, 4, 0), ("w", 2, -1, 1),
+    ("m", 0, 1, -3), ("m", 0, -1, -3), ("m", 1, 1, -3), ("m", 1, -1, -3), ("w", 2, 1, 1), ("w", 2, -1, 3),
+    ("p", 1, 0), ("p", 0, 0), ("w", 3, 2, 0), ("w", 3, -2, 0), ("m", 0, 1, -4), ("m", 0, -1, -4),
+    ("m", 1, 1, 4), ("m", 1, -1, 4), ("w", 2, 1, 3), ("w", 2, -2, 1), ("w", 2, 2, 1), ("w", 2, -2, 3),
+    ("w", 3, 3, 0), ("w", 3, -3, 0), ("s", 3, 1), ("p", 1, 1), ("w", 2, 2, 3), ("w", 2, -3, 1), ("p", 0, 1),
+    ("w", 2, 3, 1), ("w", 2, -3, 3), ("s", 3, 3), ("w", 3, 1, 1), ("w", 3, -4, 0), ("s", 3, 2),
+    ("w", 2, 3, 3), ("w", 3, -1, 1), ("p", 1, 3), ("p", 0, 3), ("s", 2, 2), ("w", 2, 4, 1), ("w", 3, -1, 3),
+    ("w", 3, 1, 3), ("w", 3, -1, 2), ("w", 3, 2, 1), ("w", 3, -2, 1), ("w", 3, 1, 2), ("w", 2, -1, 2),
+    ("p", 1, 2), ("p", 0, 2), ("w", 2, 4, 3), ("w", 3, -2, 3), ("w", 2, 1, 2), ("w", 3, -2, 2),
+    ("w", 3, 2, 3), ("w", 3, -3, 1), ("w", 3, 3, 1), ("w", 2, -2, 2), ("p", 3, 7), ("w", 3, 2, 2),
+    ("w", 3, -3, 3), ("p", 2, 7), ("w", 2, 2, 2), ("w", 3, -3, 2), ("p", 3, 1), ("w", 3, 3, 3),
+    ("w", 3, -4, 1), ("p", 2, 1), ("w", 3, 3, 2), ("w", 2, -3, 2), ("p", 3, 6), ("w", 2, 3, 2),
+    ("w", 3, -4, 3), ("p", 2, 6), ("w", 3, -4, 2), ("p", 3, 2), ("w", 2, 4, 2), ("p", 2, 2), ("p", 3, 5),
+    ("p", 2, 5), ("p", 3, 3), ("p", 2, 3), ("p", 3, 4), ("p", 2, 4),
+)
 
 
 def step_kernel(
     history,
-    table,
+    plist,
+    rdst,
+    lsrc,
+    ldst,
     rtiles,
     ltiles,
     cotangent,
-    weight,
-    bias,
+    weight_hbm,
+    bias_hbm,
     new_rows,
     grad_weight,
     grad_bias,
@@ -59,6 +88,13 @@
     (
         lists_v,
         lists_s,
+        rdst_v,
+        ldst_v,
+        lsrc_s,
+        rows_v,
+        rows_s,
+        weight,
+        bias,
         hist,
         rt,
         lt,
@@ -111,6 +147,12 @@
         return hist.at[:, pl.ds(SLICE * t, SLICE), :]
 
     load_hist = local(history, hist)
+    small = [
+        local(plist, lists_v.at[0]),
+        local(rdst, rdst_v),
+        local(ldst, ldst_v),
+        local(lsrc, lsrc_s),
+    ]
     up = lax.rem(p + 1, 128)
     down = lax.rem(p + 127, 128)
     column = [moved(me, Z, k) for k in range(1, 8)]
@@ -124,16 +166,27 @@
     greeted = [(up, f), (down, f), (p, 1 - f)] + [(d, f) for d in column + flat]
     for d in greeted:
         pl.semaphore_signal(barrier, inc=1, device_id=d, device_id_type=MESH)
-    load_rt = local(rtiles, rt)
+    order = (0, 1, 7, 2, 6, 3, 5, 4)
+
+    def load_tiles(i):
+        z = lax.rem(me[2] - order[i] + 8, 8)
+        return local(rtiles.at[:, :, z], rt.at[i % SLOTS])
+
+    tiles_in = [load_tiles(i) for i in range(SLOTS)]
     load_lt = local(ltiles, lt)
     load_cot = local(cotangent, cot)
+    load_weight = local(weight_hbm, weight)
+    load_bias = local(bias_hbm, bias)
     sums[TILES] = jnp.zeros((BLK, HALF), jnp.float32)
     load_hist.wait()
+    for copy in small:
+        copy.wait()
     pl.semaphore_wait(barrier, len(greeted))
 
     z_in = {}
     mid_in = {}
     wide_in = {}
+    far_in = {}
     last_in = {}
     list_in = []
     reach = {0: (3, 4), 1: (4, 3), 2: (4, 3), 3: (3, 4)}
@@ -153,25 +206,53 @@
     def lists_start():
         for i, axis in enumerate((X, Y)):
             for k in (1, 2, 3):
-                list_in.append(remote(table, lists_v.at[3 * i + k], axis, -k))
+                list_in.append(remote(lists_v.at[0], lists_v.at[3 * i + k], axis, -k))
+
+    def index_rows():
+        lane = lax.broadcasted_iota(jnp.int32, (1, 128), 1)
+        h = lax.rem(me[2] - lax.rem(lane, 8) + 8, 8)
+        key = LOCAL + group_rank(h) * 32 + (lane // 32) * 8 + lax.rem(lane // 8, 4) * 2
+        wanted = lists_v[0]
+        there = rdst_v[...]
+        near = jnp.concatenate([ldst_v[...], jnp.full((1, 64), -1, jnp.int32)], axis=1)
+        rows = [there[0:1], there[1:2]]
+        given = [jnp.where(wanted[c : c + 1] >= 0, rows[c], -1) for c in range(2)] + [near]
+        keys = [key, key + 1, lane]
+        none = jnp.zeros((4, 128), jnp.int32)
+        ask = jnp.concatenate(rows + [near, lane, none], axis=0).T
+        limit = jnp.concatenate(
+            keys + [jnp.full((1, 128), TILES, jnp.int32), none], axis=0
+        ).T
+        found = jnp.full((128, 128), -1, jnp.int32)
+        column_of = lax.broadcasted_iota(jnp.int32, (128, 128), 1)
+        for r in range(4):
+            best = jnp.full((128, 128), -1, jnp.int32)
+            for c in range(3):
+                match = (ask[:, r : r + 1] == given[c]) & (keys[c] < limit[:, r : r + 1])
+                best = jnp.maximum(best, jnp.where(match, keys[c], -1))
+            top = jnp.max(best, axis=1, keepdims=True)
+            found = jnp.where(column_of == r, top, found)
+        found = jnp.where(found < 0, TILES, found)
+        rows_v[...] = found.T[0:8]
 
     def lists_end():
+        local(rows_v, rows_s).wait()
         for copy in list_in:
             copy.wait_recv()
         local(lists_v, lists_s).wait()
 
-    def half_forward_first(t):
-        a = KINDS[t][0]
+    def half_forward_first(t, d):
+        here = d % 4
+        part_of = pl.ds(0 if d == 1 else 4, 4)
         ring = sets[t][0]
-        mid_in[t, 1].wait_recv()
-        u = remote(ring.at[1, pl.ds(0, 4)], ring.at[2, pl.ds(0, 4)], a, 1)
-        mid_in[t, -1].wait_recv()
-        v = remote(ring.at[3, pl.ds(4, 4)], ring.at[2, pl.ds(4, 4)], a, -1)
-        mid_in[t, 2] = (u, v)
+        mid_in[t, d].wait_recv()
+        far_in[t, d] = remote(ring.at[here, part_of], ring.at[2, part_of], KINDS[t][0], d)
 
     def first_end(t):
-        for copy in mid_in[t, 2]:
-            copy.wait_recv()
+        for d in (1, -1):
+            copy = far_in.pop((t, d), None)
+            if copy is not None:
+                copy.wait_recv()
 
     def z_arrival(t, h):
         z_in[t, h].wait_recv()
@@ -183,28 +264,27 @@
         for e in (1, -1):
             mid_in[t, e, h] = remote(here, sets[t][e % 4].at[h % 8], KINDS[t][1], e)
 
-    def half_forward(t, h):
-        b = KINDS[t][1]
-        s = h % 8
-        mid_in[t, 1, h].wait_recv()
-        u = remote(sets[t][1].at[s, pl.ds(0, 4)], sets[t][2].at[s, pl.ds(0, 4)], b, 1)
-        mid_in[t, -1, h].wait_recv()
-        v = remote(sets[t][3].at[s, pl.ds(4, 4)], sets[t][2].at[s, pl.ds(4, 4)], b, -1)
-        mid_in[t, 2, h] = (u, v)
+    def half_forward(t, e, h):
+        q = h % 8
+        half = pl.ds(0 if e == 1 else 4, 4)
+        mid_in[t, e, h].wait_recv()
+        far_in[t, e, h] = remote(
+            sets[t][e % 4].at[q, half], sets[t][2].at[q, half], KINDS[t][1], e
+        )
 
     def half_end(t):
         for h in (0, 1, -1, 2, -2, 3, -3, (-4, 4)[t]):
-            for copy in mid_in[t, 2, h]:
-                copy.wait_recv()
+            for e in (1, -1):
+                far_in[t, e, h].wait_recv()
 
     def wide_start(t, q):
+        if q == 2:
+            first_end(t)
         source = own(t) if q == 0 else sets[t][0].at[q]
         for d in (1, -1):
             wide_in[t, d, q] = remote(source, sets[t][d % 8].at[q], Z, d)
 
     def wide_arrival(t, h, q):
-        if (t, h, q) not in wide_in:
-            return
         wide_in[t, h, q].wait_recv()
         d = 1 if h > 0 else -1
         limit = reach[t][0] if h > 0 else reach[t][1]
@@ -215,6 +295,10 @@
 
     def pack(t, g):
         a, b, c = KINDS[t]
+        if t > 1 and g == 0:
+            first_end(t)
+        if t < 2 and g == 2:
+            half_end(t)
         n = SIZES[a]
         source = sets[t][g]
         target = packs[t]
@@ -251,43 +335,45 @@
             copy.wait_recv()
 
     def local_tiles(start, stop):
+        if start == 0:
+            load_lt.wait()
+
         def eight(i, carry):
             values = []
             for j in range(8):
                 k = i * 8 + j
                 values.append(
                     jnp.dot(
-                        lt[k], hist[lists_s[0, 5, k]], preferred_element_type=jnp.float32
+                        lt[k], hist[lsrc_s[0, k]], preferred_element_type=jnp.float32
                     )
                 )
             for j in range(8):
                 k = i * 8 + j
-                sums[k] = sums[lists_s[0, 4, k]] + values[j]
+                sums[k] = sums[rows_s[2, k]] + values[j]
             return carry
 
         lax.fori_loop(start, stop, eight, 0)
 
-    order = (0, 1, 7, 2, 6, 3, 5, 4)
-
-    def remote_tiles(g):
-        first = LOCAL + 32 * order.index(g)
+    def remote_tiles(n):
+        g = order[n]
+        first = LOCAL + 32 * n
+        tiles = rt.at[n % SLOTS]
         z = lax.rem(me[2] - g + 8, 8)
 
         def eight(i, carry):
             values = []
             for j in range(4):
-                o = i * 32 + j * 8 + z
                 for c in range(2):
                     values.append(
                         jnp.dot(
-                            rt[o, c], pulled[i, j, z, c], preferred_element_type=jnp.float32
+                            tiles[i, j, c], pulled[i, j, z, c], preferred_element_type=jnp.float32
                         )
                     )
             for j in range(4):
                 o = i * 32 + j * 8 + z
                 for c in range(2):
                     sums[first + i * 8 + j * 2 + c] = (
-                        sums[lists_s[0, 2 + c, o]] + values[2 * j + c]
+                        sums[rows_s[c, o]] + values[2 * j + c]
                     )
             return carry
 
@@ -298,113 +384,62 @@
     z_start(1)
     first_start(2)
     first_start(3)
-    lists_start()
     mid_start(0)
     mid_start(1)
+    lists_start()
     for t in range(4):
         sets[t][0][0] = hist[:, SLICE * t : SLICE * (t + 1), :]
-    lists_v[0] = table[...]
-    wide_start(2, 0)
-    wide_start(3, 0)
-    half_forward_first(2)
-    half_forward_first(3)
-    for h in (1, -1):
-        for t in (0, 1):
-            z_arrival(t, h)
-    half_forward(0, 0)
-    half_forward(1, 0)
-    lists_end()
-    first_end(2)
-    first_end(3)
-    pack(2, 0)
-    pack(3, 0)
-    wide_start(2, 1)
-    wide_start(3, 1)
-    for h in (2, -2):
-        for t in (0, 1):
-            z_arrival(t, h)
-    for h in (1, -1):
-        for t in (0, 1):
-            half_forward(t, h)
-    wide_start(2, 3)
-    wide_start(3, 3)
-    for h in (3, -3):
-        for t in (0, 1):
-            z_arrival(t, h)
-    wide_start(2, 2)
-    wide_start(3, 2)
-    for h in (1, -1):
-        for t in (2, 3):
-            wide_arrival(t, h, 0)
-    for h in (2, -2):
-        for t in (0, 1):
-            half_forward(t, h)
-    for h in (1, -1):
-        for t in (2, 3):
-            wide_arrival(t, h, 1)
-    z_arrival(0, -4)
-    z_arrival(1, 4)
-    for h in (3, -3):
-        for t in (0, 1):
-            half_forward(t, h)
-    pack(0, 0)
-    pack(1, 0)
-    for h in (1, -1):
-        for t in (2, 3):
-            wide_arrival(t, h, 3)
-    half_forward(0, -4)
-    half_forward(1, 4)
-    for g in (1, 3):
-        pack(0, g)
-        pack(1, g)
-    for h in (1, -1):
-        for t in (2, 3):
-            wide_arrival(t, h, 2)
-    for g in (1, 7):
-        pack(2, g)
-        pack(3, g)
-    for t in (0, 1):
-        half_end(t)
-        pack(t, 2)
-    load_lt.wait()
-    for s in (2, 3, 4):
-        for i, q in enumerate((0, 1, 3, 2)):
-            for h in (s, -s):
-                for t in (2, 3):
-                    wide_arrival(t, h, q)
-            if s == 2:
-                local_tiles(2 * i, 2 * i + 2)
-        for h in (s, -s):
-            for t in (2, 3):
-                if (t, h, 0) in wide_in:
-                    pack(t, h % 8)
-    load_rt.wait()
+    index_rows()
+    steps = {
+        "z": z_arrival,
+        "m": half_forward,
+        "f": half_forward_first,
+        "s": wide_start,
+        "w": wide_arrival,
+        "p": pack,
+    }
+    packed = 0
+    for event in EVENTS:
+        if event[0] == "p":
+            if packed == 0:
+                lists_end()
+            packed += 1
+        steps[event[0]](*event[1:])
+        if event[0] == "p" and packed > 10 and packed <= 18:
+            local_tiles(packed - 11, packed - 10)
     for t in (0, 1):
         for g in (0, 1, 3, 2):
             arrived(t, g)
-    for g in order:
+    for n, g in enumerate(order):
         arrived(2, g)
         arrived(3, g)
-        remote_tiles(g)
-
+        tiles_in[n].wait()
+        remote_tiles(n)
+        if n + SLOTS < 8:
+            tiles_in.append(load_tiles(n + SLOTS))
     load_cot.wait()
+    load_weight.wait()
+    load_bias.wait()
     shifts = []
     for t in range(NB):
-        following[t] = sums[lists_s[0, 4, 64 + NB + t]].astype(jnp.bfloat16)
+        following[t] = sums[rows_s[3, NB + t]].astype(jnp.bfloat16)
         shifts.append(send(following.at[t], coming.at[t], up, f))
     swaps = []
-    for t in range(NB):
-        mine = sums[lists_s[0, 4, 64 + t]]
-        shifts[t].wait_recv()
-        agg[t] = (mine + coming[t].astype(jnp.float32)).astype(jnp.bfloat16)
-        swaps.append(send(agg.at[t], other.at[t], p, 1 - f))
     w_mine = weight[pl.ds(pl.multiple_of(f * HALF, HALF), HALF), :]
     w_other = weight[pl.ds(pl.multiple_of((1 - f) * HALF, HALF), HALF), :]
     b = bias[...]
     g_mine = jnp.zeros((HALF, HALF), jnp.float32)
     g_other = jnp.zeros((HALF, HALF), jnp.float32)
     g_bias = jnp.zeros((8, HALF), jnp.float32)
-    for t in range(NB):
+    for u in range(NB + LAG):
+        if u < NB:
+            mine = sums[rows_s[3, u]]
+            shifts[u].wait_recv()
+            agg[u] = (mine + coming[u].astype(jnp.float32)).astype(jnp.bfloat16)
+            swaps.append(send(agg.at[u], other.at[u], p, 1 - f))
+        t = u - LAG
+        if t < 0:
+            continue
         swaps[t].wait_recv()
         a0 = agg[t]
         a1 = other[t]
@@ -453,7 +488,7 @@
         copy.wait_send()
 
 
-def step(blocks, table, rtiles, ltiles, cotangent, weight, bias):
+def step(*arrays):
     vm = pl.BlockSpec(memory_space=pltpu.VMEM)
     hbm = pl.BlockSpec(memory_space=pl.ANY)
     bf16 = jnp.bfloat16
@@ -465,17 +500,24 @@
             jax.ShapeDtypeStruct((2 * HALF, HALF), f32),
             jax.ShapeDtypeStruct((1, HALF), f32),
         ),
-        in_specs=[hbm, vm, hbm, hbm, hbm, vm, vm],
+        in_specs=[hbm] * 10,
         out_specs=(vm, vm, vm),
         scratch_shapes=[pltpu.VMEM((8, NB, SLICE, HALF), bf16)] * 8
         + [pltpu.VMEM((4, NB, SLICE, HALF), bf16)] * 16
         + [pltpu.VMEM((3, 4, 8, 2, SLICE, HALF), bf16)] * 2
         + [pltpu.VMEM((3, 8, 4, 2, SLICE, HALF), bf16)] * 2
         + [
-            pltpu.VMEM((7, 8, 128), jnp.int32),
-            pltpu.SMEM((7, 8, 128), jnp.int32),
+            pltpu.VMEM((7, 2, 128), jnp.int32),
+            pltpu.SMEM((7, 2, 128), jnp.int32),
+            pltpu.VMEM((2, 128), jnp.int32),
+            pltpu.VMEM((1, 64), jnp.int32),
+            pltpu.SMEM((1, 64), jnp.int32),
+            pltpu.VMEM((8, 128), jnp.int32),
+            pltpu.SMEM((8, 128), jnp.int32),
+            pltpu.VMEM((2 * HALF, HALF), bf16),
+            pltpu.VMEM((1, HALF), f32),
             pltpu.VMEM((NB, BLK, HALF), bf16),
-            pltpu.VMEM((128, 2, BLK, BLK), bf16),
+            pltpu.VMEM((SLOTS, 4, 4, 2, BLK, BLK), bf16),
             pltpu.VMEM((LOCAL, BLK, BLK), bf16),
             pltpu.VMEM((NB * BLK, HALF), bf16),
             pltpu.VMEM((4, 4, 8, 2, BLK, HALF), bf16),
@@ -490,43 +532,13 @@
             pltpu.VMEM((16, PIECE, HALF), f32),
             pltpu.SemaphoreType.DMA((320,)),
             pltpu.SemaphoreType.DMA((320,)),
-            pltpu.SemaphoreType.DMA((8,)),
+            pltpu.SemaphoreType.DMA((24,)),
         ],
         compiler_params=pltpu.CompilerParams(
-            collective_id=0, has_side_effects=True, vmem_limit_bytes=67043328
+            collective_id=0, has_side_effects=True, vmem_limit_bytes=51 << 20
         ),
         name="step",
-    )(blocks, table, rtiles, ltiles, cotangent, weight, bias)
-
-
-def index_table(plist, remote_dst, local_src, local_dst):
-    mz = lax.rem(lax.axis_index("dom"), 8)
-    i = jnp.arange(256, dtype=jnp.int32)
-    o = i // 2
-    h = lax.rem(mz - lax.rem(o, 8) + 8, 8)
-    key = LOCAL + group_rank(h) * 32 + (o // 32) * 8 + lax.rem(o // 8, 4) * 2 + lax.rem(i, 2)
-    near = jnp.arange(LOCAL, dtype=jnp.int32)
-    dst = jnp.where(plist.reshape(-1) >= 0, remote_dst.reshape(-1), -1)
-    dst = jnp.concatenate([local_dst.reshape(-1), dst])
-    keys = jnp.concatenate([near, key])
-    want = jnp.concatenate(
-        [remote_dst.T.reshape(-1), local_dst.reshape(-1), jnp.arange(16, dtype=jnp.int32)]
-    )
-    limit = jnp.concatenate(
-        [key.reshape(128, 2).T.reshape(-1), near, jnp.full((16,), TILES, jnp.int32)]
-    )
-    match = (want[:, None] == dst[None, :]) & (keys[None, :] < limit[:, None])
-    before = jnp.max(jnp.where(match, keys[None, :], -1), axis=1)
-    before = jnp.where(before < 0, TILES, before)
-    return jnp.concatenate(
-        [
-            plist.T.reshape(-1),
-            before,
-            jnp.zeros((48,), jnp.int32),
-            local_src.reshape(-1),
-            jnp.zeros((64 + 256,), jnp.int32),
-        ]
-    ).reshape(8, 128)
+    )(*arrays)
 
 
 def per_device(
@@ -541,11 +553,13 @@
     bias,
     cotangent,
 ):
-    table = index_table(pull_list[0], remote_dst[0], local_src, local_dst)
     new_rows, grad_weight, grad_bias = step(
         history.reshape(NB, BLK, HALF),
-        table,
-        remote_tiles[0],
+        pull_list[0].T,
+        remote_dst[0].T,
+        local_src,
+        local_dst,
+        remote_tiles[0].reshape(4, 4, 8, 2, BLK, BLK),
         local_tiles,
         cotangent,
         weight,

time: 119 us -> 118 us (level)
  other arithmetic: 2.58 us -> 0 us
  local copies, waits for them, and re-layouts: 6.02 us -> 7.92 us
    unnamed x3 -> x19, local copies, waits for them, and re-layouts: 4.41 us -> 7.92 us
    concatenate x4 -> x0, other arithmetic: 1.66 us -> none  [the longest x1 0.77 us: index_table(): jnp.concatenate([remote_dst.T.reshape(-1), local_dst.reshape(-1), jnp.ara...]
    concatenate x1 -> x0, local copies, waits for them, and re-layouts: 1.35 us -> none  [index_table(): jnp.concatenate([plist.T.reshape(-1), before, jnp.zeros((48,), jnp.int32)...]
where the time goes in v3:
time: 118 us; the launch traced here: 117 us
  Pallas kernels  109 us (92%)
  local copies, waits for them, and re-layouts  7.92 us (7%)
    pallas_call x1, Pallas kernels, step(): pl.pallas_call(step_kernel, out_shape=(jax.ShapeDtypeStruct((NB * BLK, HA...  109 us
    unnamed x19, local copies, waits for them, and re-layouts  7.92 us

profile of v3, /device:TPU:32, one launch (start us, length us, event | category | flops | bytes accessed | tf_op | source)
XLA Modules:
  0.0 117.3 jit_solution(2735116449042541831)
XLA Ops:
  0.6 0.0 copy-start
  0.6 0.9 copy-done
  1.6 0.0 copy-start.1
  1.6 0.9 copy-done.1
  2.5 0.0 copy-start.2
  2.5 0.8 copy-done.2
  3.4 0.0 copy-start.3
  3.4 0.7 copy-done.3
  4.1 0.0 copy-start.4
  4.1 0.7 copy-done.4
  4.7 0.0 copy-start.5
  4.7 0.7 copy-done.5
  5.4 0.0 copy-start.6
  5.4 0.7 copy-done.6
  6.0 0.0 copy-start.7
  6.0 0.7 copy-done.7
  6.7 108.7 %step.1 = (bf16[1024,128]{1,0:T(8,128)(2,1)S(1)}, f32[256,128]{1,0:T(8,128)S(1)}, f32[1,128]{1,0:T(1,128)S(1)}) custom-call(bf16[8,128,128]{2,1,0:T(8,128)(2,1)S(1)} %bitcast.10, s32[2,128]{1,0:T(2,128)S(1)} %bitcast.11, s32[2,128]{1,0:T(2,128)S(1)} %bitcast.12, s32[1,64]{1,0:T(1,128)S(1)} %copy-done.5, s32[1,64]{1,0:T(1,128)S(1)} %copy-done.6, ...), custom_call_target="tpu_custom_call" | custom-call | tf_op jit(solution)/shard_map/step/pallas_call | solution.py:496
  115.4 0.7 copy.16
  116.1 0.7 copy.17
  116.7 0.5 copy.18
Async XLA Ops:
  0.6 1.0 copy-start
  1.6 0.9 copy-start.1
  2.5 0.8 copy-start.2
  3.4 0.7 copy-start.3
  4.1 0.7 copy-start.4
  4.7 0.7 copy-start.5
  5.4 0.7 copy-start.6
  6.0 0.7 copy-start.7

commit v4 on v3

--- a/solution.py
+++ b/solution.py
@@ -154,7 +154,6 @@
         local(lsrc, lsrc_s),
     ]
     up = lax.rem(p + 1, 128)
-    down = lax.rem(p + 127, 128)
     column = [moved(me, Z, k) for k in range(1, 8)]
     flat = [
         lax.rem(me[0] + i, 4) * 32 + lax.rem(me[1] + j, 4) * 8 + me[2]
@@ -163,7 +162,8 @@
         if i or j
     ]
     barrier = pltpu.get_barrier_semaphore()
-    greeted = [(up, f), (down, f), (p, 1 - f)] + [(d, f) for d in column + flat]
+    near = ((X, 1), (X, 2), (X, 3), (Y, 1), (Y, 2), (Y, 3), (Z, 1), (Z, 7))
+    greeted = [(p, 1 - f)] + [(moved(me, axis, k), f) for axis, k in near]
     for d in greeted:
         pl.semaphore_signal(barrier, inc=1, device_id=d, device_id_type=MESH)
     order = (0, 1, 7, 2, 6, 3, 5, 4)
@@ -490,7 +490,7 @@
 
 def step(*arrays):
     vm = pl.BlockSpec(memory_space=pltpu.VMEM)
-    hbm = pl.BlockSpec(memory_space=pl.ANY)
+    hbm = pl.BlockSpec(memory_space=pltpu.HBM)
     bf16 = jnp.bfloat16
     f32 = jnp.float32
     return pl.pallas_call(
@@ -538,7 +538,7 @@
             collective_id=0, has_side_effects=True, vmem_limit_bytes=51 << 20
         ),
         name="step",
-    )(*arrays)
+    )(*[pltpu.with_memory_space_constraint(a, pltpu.HBM) for a in arrays])
 
 
 def per_device(

time: 118 us -> 111 us (0.941)
  local copies, waits for them, and re-layouts: 7.92 us -> 1.87 us
    unnamed x19 -> x3, local copies, waits for them, and re-layouts: 7.92 us -> 1.87 us
where the time goes in v4:
time: 111 us; the launch traced here: 110 us
  Pallas kernels  108 us (97%)
  local copies, waits for them, and re-layouts  1.87 us (2%)
    pallas_call x1, Pallas kernels, step(): pl.pallas_call(step_kernel, out_shape=(jax.ShapeDtypeStruct((NB * BLK, HA...  108 us

profile of v4, /device:TPU:32, one launch (start us, length us, event | category | flops | bytes accessed | tf_op | source)
XLA Modules:
  0.0 110.2 jit_solution(5101644249062237042)
XLA Ops:
  0.6 107.7 %step.1 = (bf16[1024,128]{1,0:T(8,128)(2,1)S(1)}, f32[256,128]{1,0:T(8,128)S(1)}, f32[1,128]{1,0:T(1,128)S(1)}) custom-call(bf16[8,128,128]{2,1,0:T(8,128)(2,1)} %bitcast.12, s32[2,128]{1,0:T(2,128)} %bitcast.13, s32[2,128]{1,0:T(2,128)} %bitcast.14, s32[1,64]{1,0:T(1,128)} %lsrc.1, s32[1,64]{1,0:T(1,128)} %ldst.1, ...), custom_call_target="tpu_custom_call" | custom-call | tf_op jit(solution)/shard_map/step/pallas_call | solution.py:496
  108.3 0.7 copy.16
  109.0 0.7 copy.17
  109.7 0.5 copy.18

commit v5 on v4

--- a/solution.py
+++ b/solution.py
@@ -154,12 +154,13 @@
         local(lsrc, lsrc_s),
     ]
     up = lax.rem(p + 1, 128)
-    column = [moved(me, Z, k) for k in range(1, 8)]
+    column = [moved(me, Z, k) for k in (4, 3, 5, 2, 6, 1, 7)]
     flat = [
         lax.rem(me[0] + i, 4) * 32 + lax.rem(me[1] + j, 4) * 8 + me[2]
-        for i in range(4)
-        for j in range(4)
-        if i or j
+        for i, j in (
+            ((2, 2), (2, 1), (1, 2), (2, 3), (3, 2), (1, 1), (1, 3), (3, 1), (3, 3))
+            + ((2, 0), (0, 2), (1, 0), (0, 1), (3, 0), (0, 3))
+        )
     ]
     barrier = pltpu.get_barrier_semaphore()
     near = ((X, 1), (X, 2), (X, 3), (Y, 1), (Y, 2), (Y, 3), (Z, 1), (Z, 7))
@@ -467,7 +468,7 @@
     spot = me[0] * 4 + me[1]
     ins = [send(terms.at[d // 8], part.at[i], d, f) for i, d in enumerate(flat)]
     total = terms[spot]
-    for i in range(15):
+    for i in reversed(range(15)):
         ins[i].wait_recv()
         total = total + part[i]
     column_sums[me[2]] = total
@@ -541,6 +542,30 @@
     )(*[pltpu.with_memory_space_constraint(a, pltpu.HBM) for a in arrays])
 
 
+def place_kernel(*refs):
+    sems = refs[6]
+    copies = [
+        pltpu.make_async_copy(refs[i], refs[3 + i], sems.at[i]) for i in range(3)
+    ]
+    for copy in copies:
+        copy.start()
+    for copy in copies:
+        copy.wait()
+
+
+def place(*arrays):
+    anywhere = pl.BlockSpec(memory_space=pl.ANY)
+    return pl.pallas_call(
+        place_kernel,
+        out_shape=tuple(jax.ShapeDtypeStruct(a.shape, a.dtype) for a in arrays),
+        in_specs=[anywhere] * 3,
+        out_specs=(anywhere,) * 3,
+        scratch_shapes=[pltpu.SemaphoreType.DMA((3,))],
+        compiler_params=pltpu.CompilerParams(vmem_limit_bytes=4 << 20),
+        name="place",
+    )(*arrays)
+
+
 def per_device(
     history,
     pull_list,
@@ -565,6 +590,7 @@
         weight,
         bias.reshape(1, HALF),
     )
+    new_rows, grad_weight, grad_bias = place(new_rows, grad_weight, grad_bias)
     return new_rows, grad_weight, grad_bias.reshape(HALF)
 
 

time: 111 us -> 108 us (0.973)
  local copies, waits for them, and re-layouts: 1.87 us -> 0 us
    unnamed x3 -> x0, local copies, waits for them, and re-layouts: 1.87 us -> none
where the time goes in v5:
time: 108 us
  Pallas kernels  107 us (99%)
    pallas_call x1, Pallas kernels, step(): pl.pallas_call(step_kernel, out_shape=(jax.ShapeDtypeStruct((NB * BLK, HA...  107 us

profile of v5, /device:TPU:32, one launch (start us, length us, event | category | flops | bytes accessed | tf_op | source)
XLA Modules:
  0.0 108.1 jit_solution(15664120556600463824)
XLA Ops:
  0.6 106.7 %step.1 = (bf16[1024,128]{1,0:T(8,128)(2,1)S(1)}, f32[256,128]{1,0:T(8,128)S(1)}, f32[1,128]{1,0:T(1,128)S(1)}) custom-call(bf16[8,128,128]{2,1,0:T(8,128)(2,1)} %bitcast.11, s32[2,128]{1,0:T(2,128)} %bitcast.12, s32[2,128]{1,0:T(2,128)} %bitcast.13, s32[1,64]{1,0:T(1,128)} %lsrc.1, s32[1,64]{1,0:T(1,128)} %ldst.1, ...), custom_call_target="tpu_custom_call" | custom-call | tf_op jit(solution)/shard_map/step/pallas_call | solution.py:497
  107.3 0.8 place.1

commit v6 on v5

--- a/solution.py
+++ b/solution.py
@@ -35,6 +35,7 @@
 
 
 PIECE = 24
+ROWS = pl.ds(0, 17)
 ROOT = 0.7978845608028654
 CUBIC = 0.044715
 TILES = 320
@@ -378,7 +379,8 @@
                     )
             return carry
 
-        lax.fori_loop(0, 4, eight, 0)
+        for i in range(4):
+            eight(i, 0)
 
 
     z_start(0)
@@ -463,28 +465,28 @@
     terms[pl.ds(f * 8, 8), 0:16, :] = g_mine.reshape(8, 16, HALF)
     terms[pl.ds((1 - f) * 8, 8), 0:16, :] = g_other.reshape(8, 16, HALF)
     terms[:, 16:24, :] = jnp.zeros((16, 8, HALF), jnp.float32)
-    terms[0, 16:24, :] = g_bias
+    terms[0, 16:17, :] = jnp.sum(g_bias, axis=0, keepdims=True)
 
     spot = me[0] * 4 + me[1]
-    ins = [send(terms.at[d // 8], part.at[i], d, f) for i, d in enumerate(flat)]
-    total = terms[spot]
+    ins = [send(terms.at[d // 8, ROWS], part.at[i, ROWS], d, f) for i, d in enumerate(flat)]
+    total = terms[spot, 0:17]
     for i in reversed(range(15)):
         ins[i].wait_recv()
-        total = total + part[i]
-    column_sums[me[2]] = total
-    ins = [send(column_sums.at[me[2]], column_sums.at[me[2]], d, f) for d in column]
+        total = total + part[i, 0:17]
+    column_sums[me[2], 0:17] = total
+    ins = [send(column_sums.at[me[2], ROWS], column_sums.at[me[2], ROWS], d, f) for d in column]
     for copy in ins:
         copy.wait_recv()
-    total = column_sums[0]
+    total = column_sums[0, 0:17]
     for k in range(1, 8):
-        total = total + column_sums[k]
-    final[spot] = total
-    ins = [send(final.at[spot], final.at[spot], d, f) for d in flat]
+        total = total + column_sums[k, 0:17]
+    final[spot, 0:17] = total
+    ins = [send(final.at[spot, ROWS], final.at[spot, ROWS], d, f) for d in flat]
     for copy in ins:
         copy.wait_recv()
     for k in range(16):
         grad_weight[16 * k : 16 * (k + 1), :] = final[k, 0:16, :]
-    grad_bias[...] = jnp.sum(final[0, 16:24, :], axis=0, keepdims=True)
+    grad_bias[...] = final[0, 16:17, :]
     for copy in remote_copies:
         copy.wait_send()
 

time: 108 us -> 106 us (0.981)
    pallas_call x1, Pallas kernels: 107 us -> 105 us  [step(): pl.pallas_call(step_kernel, out_shape=(jax.ShapeDtypeStruct((NB * BLK, HA...]
where the time goes in v6:
time: 106 us
  Pallas kernels  106 us (100%)
    pallas_call x1, Pallas kernels, step(): pl.pallas_call(step_kernel, out_shape=(jax.ShapeDtypeStruct((NB * BLK, HA...  105 us

profile of v6, /device:TPU:32, one launch (start us, length us, event | category | flops | bytes accessed | tf_op | source)
XLA Modules:
  0.0 106.4 jit_solution(7103021242249336220)
XLA Ops:
  0.6 105.0 %step.1 = (bf16[1024,128]{1,0:T(8,128)(2,1)S(1)}, f32[256,128]{1,0:T(8,128)S(1)}, f32[1,128]{1,0:T(1,128)S(1)}) custom-call(bf16[8,128,128]{2,1,0:T(8,128)(2,1)} %bitcast.11, s32[2,128]{1,0:T(2,128)} %bitcast.12, s32[2,128]{1,0:T(2,128)} %bitcast.13, s32[1,64]{1,0:T(1,128)} %lsrc.1, s32[1,64]{1,0:T(1,128)} %ldst.1, ...), custom_call_target="tpu_custom_call" | custom-call | tf_op jit(solution)/shard_map/step/pallas_call | solution.py:499
  105.6 0.8 place.1
